TPU v7x, 256 devices: a whole 4x4x8 slice. The times are simulated.
256 devices in a mesh: gx: 16 (over z_hi, y, core), gy: 4 (over z_lo), gz: 4 (over x).
Axes of the slice: x: 4, y: 4, z: 8 (z_hi: 2, z_lo: 4; z = z_hi * 4 + z_lo), core: 2. Of those that a mesh axis runs over, the one named last changes fastest.
Arguments:
- offsets: float32 [3, 64, 16, 16, 128], P(None, 'gx', 'gy', 'gz'), may hold values from 0 to 1
- burgers: float32 [3, 64, 16, 16, 128], P(None, 'gx', 'gy', 'gz'), may hold values from -6 to 6
- lines: float32 [3, 64, 16, 16, 128], P(None, 'gx', 'gy', 'gz'), may hold values from -3 to 3
- counts: int32 [64, 16, 16], P('gx', 'gy', 'gz'), may hold values from 1 to 128
- connect: int32 [2, 64, 16, 16, 128], P(None, 'gx', 'gy', 'gz'), may hold values from 0 to 8191
- node_pos: float32 [3, 16, 4, 4, 8192], P(None, 'gx', 'gy', 'gz'), may hold values from -6 to 6
- drag: float32 [16, 4, 4, 8192], P('gx', 'gy', 'gz'), may hold values from 0.5 to 4
- stress: float32 [3, 3], replicated, may hold values from -1 to 1
- shifts: int32 [2, 16, 4, 4], replicated, may hold values from 0 to 512, as said below
Outputs:
- migrated: float32 [6, 16, 4, 4, 9216], P(None, 'gx', 'gy', 'gz')
Inputs may be any that keep to these rules, and one draw needn't show every extreme that they name: shifts[0] of the last domain along gx is 0 and shifts[1] of the first is 0; 512 is reached by both rows in every draw.
All inputs are finite; a program needn't handle non-finite values.
Results may differ from a plain program's by a relative error of at most 0.0003.
Values sent between devices are 32-bit elements; how exact they have to be, the bound alone decides.
No kernel may reach another device: no remote copies, remote signals or barrier semaphores. Data moves between devices by JAX's collectives and lax.ppermute only.
A program may use at most 64 MiB of HBM per device.

v0:
```python
import jax
import jax.numpy as jnp
from jax import lax
from jax.sharding import PartitionSpec as P

MIG = 512


SOFTEN_NEAR = 0.25
SOFTEN_FAR = 4.0
NEAR_SCALE = 0.0625
FAR_SCALE = 0.03125
TIME_STEP = 0.1
NEIGHBOURS = ((1, 0, 0), (-1, 0, 0), (0, 1, 0), (0, -1, 0), (0, 0, 1), (0, 0, -1))


def extended(array, sides, width):
    edges = {}
    for axis, dim in sides:
        count, length = (lax.axis_size(axis), array.shape[dim])
        up = [(i, (i + 1) % count) for i in range(count - 1)]
        last = lax.slice_in_dim(array, length - width, length, axis=dim)
        leading = lax.slice_in_dim(array, 0, width, axis=dim)
        edges[dim] = (
            lax.ppermute(last, axis, up),
            lax.ppermute(leading, axis, [(b, a) for a, b in up]),
        )
    done = []
    for _, dim in sides:
        low, high = edges[dim]
        around = [(width, width) if d in done else (0, 0) for d in range(array.ndim)]
        array = jnp.concatenate([jnp.pad(low, around), array, jnp.pad(high, around)], axis=dim)
        done.append(dim)
    return array


def passed_along(array, axis, by):
    count = lax.axis_size(axis)
    pairs = [(i, i + by) for i in range(count) if 0 <= i + by < count]
    return lax.ppermute(array, axis, pairs)


def as_index(value):
    return jnp.asarray(value).astype(jnp.int32)


def pair_term(target, source, offset):
    deltas = [
        target[axis_id][..., :, None] - source[axis_id][..., None, :] - float(offset[axis_id])
        for axis_id in range(3)
    ]
    radius = deltas[0] * deltas[0] + deltas[1] * deltas[1] + deltas[2] * deltas[2] + SOFTEN_NEAR
    inverse = lax.rsqrt(radius)
    burgers_dot = (
        target[3][..., :, None] * source[3][..., None, :]
        + target[4][..., :, None] * source[4][..., None, :]
        + target[5][..., :, None] * source[5][..., None, :]
    )
    line_dot = (
        target[6][..., :, None] * source[6][..., None, :]
        + target[7][..., :, None] * source[7][..., None, :]
        + target[8][..., :, None] * source[8][..., None, :]
    )
    weight = burgers_dot * line_dot * inverse * inverse * inverse
    return jnp.stack([jnp.sum(weight * deltas[axis_id], axis=-1) for axis_id in range(3)])


def far_stress(moments, centers, cells):
    distance = SOFTEN_FAR + jnp.zeros((cells.shape[1], centers.shape[1]), jnp.float32)
    for axis_id in range(3):
        gap = cells[axis_id][:, None] - centers[axis_id][None, :]
        distance = distance + gap * gap
    weights = lax.rsqrt(distance)
    return jnp.dot(
        moments, weights.T, precision=lax.Precision.HIGHEST, preferred_element_type=jnp.float32
    )


def segment_force(target, sigma):
    burgers = target[3:6]
    line = target[6:9]
    pulled = [
        sigma[row, 0][..., None] * burgers[0]
        + sigma[row, 1][..., None] * burgers[1]
        + sigma[row, 2][..., None] * burgers[2]
        for row in range(3)
    ]
    return jnp.stack(
        [
            pulled[1] * line[2] - pulled[2] * line[1],
            pulled[2] * line[0] - pulled[0] * line[2],
            pulled[0] * line[1] - pulled[1] * line[0],
        ]
    )


def coarse_moments(stacked):
    product = jnp.einsum(
        "axyzk,bxyzk->abxyz", stacked[3:6], stacked[6:9], precision=lax.Precision.HIGHEST
    )
    sx, sy, sz = (product.shape[2], product.shape[3], product.shape[4])
    return product.reshape(9, sx // 2, 2, sy // 2, 2, sz // 2, 2).sum(axis=(2, 4, 6))


def window(padded, starts, grid):
    return lax.slice(
        padded,
        (0, starts[0], starts[1], starts[2], 0),
        (
            padded.shape[0],
            starts[0] + grid[0],
            starts[1] + grid[1],
            starts[2] + grid[2],
            padded.shape[4],
        ),
    )


def shards(offsets, burgers, lines, counts, connect, node_pos, drag, stress, shifts):
    size_x, size_y, size_z, slots = (
        offsets.shape[1],
        offsets.shape[2],
        offsets.shape[3],
        offsets.shape[4],
    )
    grid = (size_x, size_y, size_z)
    index_x = lax.axis_index("gx")
    index_y = lax.axis_index("gy")
    index_z = lax.axis_index("gz")
    count_x = lax.axis_size("gx")
    count_y = lax.axis_size("gy")
    count_z = lax.axis_size("gz")
    mask = (lax.broadcasted_iota(jnp.int32, grid + (slots,), 3) < counts[..., None]).astype(
        jnp.float32
    )
    stacked = jnp.concatenate([offsets, burgers * mask[None], lines], axis=0)
    near = pair_term(stacked, stacked, (0, 0, 0))
    padded = extended(stacked, (("gx", 1), ("gy", 2), ("gz", 3)), 1)
    for offset in NEIGHBOURS:
        source = window(padded, (1 + offset[0], 1 + offset[1], 1 + offset[2]), grid)
        near = near + pair_term(stacked, source, offset)
    own_moments = coarse_moments(stacked)
    half_x, half_y, half_z = (size_x // 2, size_y // 2, size_z // 2)
    whole = jnp.zeros((9, count_x * half_x, count_y * half_y, count_z * half_z), jnp.float32)
    corner = (
        as_index(0),
        as_index(index_x * half_x),
        as_index(index_y * half_y),
        as_index(index_z * half_z),
    )
    whole = lax.dynamic_update_slice(whole, own_moments, corner)
    whole = lax.psum(whole, ("gx", "gy", "gz"))
    moments = whole.reshape(9, -1)
    coarse_grid = (count_x * half_x, count_y * half_y, count_z * half_z)
    centers = jnp.stack(
        [
            (2 * lax.broadcasted_iota(jnp.int32, coarse_grid, axis_id) + 1)
            .astype(jnp.float32)
            .reshape(-1)
            for axis_id in range(3)
        ]
    )
    starts = (index_x * size_x, index_y * size_y, index_z * size_z)
    cells = jnp.stack(
        [
            (lax.broadcasted_iota(jnp.int32, grid, axis_id) + starts[axis_id])
            .astype(jnp.float32)
            .reshape(-1)
            + 0.5
            for axis_id in range(3)
        ]
    )
    sigma = (
        FAR_SCALE * far_stress(moments, centers, cells).reshape(3, 3, size_x, size_y, size_z)
        + stress[:, :, None, None, None]
    )
    total = NEAR_SCALE * near + segment_force(stacked, sigma)
    nodes = node_pos.shape[4]
    margin = MIG
    halves = 0.5 * total.reshape(3, -1)
    values = jnp.concatenate([halves, halves], axis=1).T
    node_force = jax.ops.segment_sum(values, connect.reshape(-1), num_segments=nodes).T
    velocity = node_force / drag.reshape(1, nodes)
    fields = jnp.concatenate([node_pos.reshape(3, nodes) + TIME_STEP * velocity, velocity], axis=0)
    from_below = passed_along(fields[:, nodes - margin :], "gx", 1)
    from_above = passed_along(fields[:, :margin], "gx", -1)
    sectioning = jnp.concatenate([from_below, fields, from_above], axis=1)
    capacity = sectioning.shape[1]
    up_own = shifts[0][index_x, index_y, index_z]
    down_own = shifts[1][index_x, index_y, index_z]
    up_prev = jnp.where(index_x > 0, shifts[0][jnp.maximum(index_x - 1, 0), index_y, index_z], 0)
    down_next = jnp.where(
        index_x < count_x - 1, shifts[1][jnp.minimum(index_x + 1, count_x - 1), index_y, index_z], 0
    )
    position = lax.broadcasted_iota(jnp.int32, (capacity,), 0)
    kept = nodes - up_own - down_own
    source = jnp.where(
        position < up_prev,
        margin - up_prev + position,
        jnp.where(
            position < up_prev + kept,
            margin + down_own + position - up_prev,
            margin + nodes + position - up_prev - kept,
        ),
    )
    source = jnp.clip(source, 0, capacity - 1)
    live = position < up_prev + kept + down_next
    result = jnp.where(live[None], jnp.take(sectioning, source, axis=1), 0.0)
    return result.reshape(6, 1, 1, 1, capacity)


def solution(mesh):
    return jax.shard_map(
        shards,
        mesh=mesh,
        in_specs=(
            P(None, "gx", "gy", "gz", None),
            P(None, "gx", "gy", "gz", None),
            P(None, "gx", "gy", "gz", None),
            P("gx", "gy", "gz"),
            P(None, "gx", "gy", "gz", None),
            P(None, "gx", "gy", "gz", None),
            P("gx", "gy", "gz", None),
            P(),
            P(),
        ),
        out_specs=P(None, "gx", "gy", "gz", None),
        check_vma=False,
    )
```

profile of v0, /device:TPU:25, one launch (start us, length us, event | category | flops | bytes accessed | tf_op | source)
XLA Modules:
  0.0 551.8 jit_solution(7163593211647792578)
XLA Ops:
  7.4 0.9 broadcast_multiply_fusion
  8.3 1.5 convolution_bitcast_fusion
  10.9 1.3 dot_general.9
  12.2 1.0 pad_maximum_fusion
  13.3 2.6 collective-permute-start
  15.9 9.0 %collective-permute-start.1 = (f32[9,1,4,4,128]{4,3,2,1,0:T(4,128)S(1)}, f32[9,1,4,4,128]{4,3,2,1,0:T(4,128)S(1)}, u32[]{:S(2)}, u32[]{:S(2)}) collective-permute-start(f32[9,1,4,4,128]{4,3,2,1,0:T(4,128)S(1)} %get-tuple-element.96), channel_id=1, source_target_pairs={{0,16},{16,32},{32,48},{48,64},{64,80},{80,96},{96,112},{112,128},... | collective-permute-start | bytes 221192 | tf_op jit(solution)/shard_map/ppermute | solution.py:25
  24.9 1.3 collective-permute-start.2
  26.2 4.2 collective-permute-start.3
  30.5 1.3 collective-permute-start.4
  36.7 2.6 copy.31
  39.9 220.0 %all-reduce.6.cloned.1.call-done = f32[3,3,2048]{2,1,0:T(4,128)} async-done(((f32[3,3,2048]{2,1,0:T(4,128)}), f32[3,3,2048]{2,1,0:T(4,128)}) %all-reduce.6.cloned.1.call-update) | async-done | bytes 73744 | tf_op jit(solution)/shard_map/psum | solution.py:152
  259.9 8.4 %fusion.46 = f32[3,3,4,4,4]{4,1,3,2,0:T(4,128)S(1)} fusion(f32[2048]{0:T(1024)S(1)} %convert_element_type.81, f32[4]{0:T(128)S(1)} %get-tuple-element.127, f32[2048]{0:T(1024)S(1)} %convert_element_type.79, f32[4]{0:T(128)S(1)} %get-tuple-element.128, f32[2048]{0:T(1024)S(1)} %convert_element_type.76, f32[4]{0:T(128)S(1)} %convert_add_fusion.2, ...), kind=kOutput, calls=%fused_computation.106 | convolution fusion | flops 15336576 | bytes 100692 | tf_op jit(solution)/shard_map/dot_general | solution.py:74
  268.3 3.5 collective-permute-start.5
  272.0 1.3 collective-permute-done.5
  274.2 15.1 %multiply_reduce_fusion.5 = (f32[4,4,4,128]{3,2,1,0:T(4,128)S(1)}, f32[4,4,4,128]{3,2,1,0:T(4,128)S(1)}, f32[4,4,4,128]{3,2,1,0:T(4,128)S(1)}) fusion(f32[4,4,4,128]{3,2,1,0:T(4,128)S(1)} %get-tuple-element.77, f32[4,4,4,128]{3,2,1,0:T(4,128)S(1)} %get-tuple-element.104, f32[4,4,4,128]{3,2,1,0:T(4,128)S(1)} %get-tuple-element.75, ...), kind=kLoop, calls=%fused_computation.96 | loop fusion | flops 31432704 | bytes 688128 | tf_op jit(solution)/shard_map/reduce_sum | solution.py:65
  289.4 15.1 %multiply_reduce_fusion.4 = (f32[4,4,4,128]{3,2,1,0:T(4,128)S(1)}, f32[4,4,4,128]{3,2,1,0:T(4,128)S(1)}, f32[4,4,4,128]{3,2,1,0:T(4,128)S(1)}) fusion(f32[4,4,4,128]{3,2,1,0:T(4,128)S(1)} %get-tuple-element.85, f32[4,4,4,128]{3,2,1,0:T(4,128)S(1)} %get-tuple-element.104, f32[4,4,4,128]{3,2,1,0:T(4,128)S(1)} %get-tuple-element.83, ...), kind=kLoop, calls=%fused_computation.94 | loop fusion | flops 31432704 | bytes 688128 | tf_op jit(solution)/shard_map/reduce_sum | solution.py:65
  304.6 15.0 %fusion.24 = (f32[4,4,4,128]{3,2,1,0:T(4,128)S(1)}, f32[4,4,4,128]{3,2,1,0:T(4,128)S(1)}, f32[4,4,4,128]{3,2,1,0:T(4,128)S(1)}) fusion(f32[4,4,4,128]{3,2,1,0:T(4,128)S(1)} %get-tuple-element.58, f32[4,4,4,128]{3,2,1,0:T(4,128)S(1)} %get-tuple-element.104, f32[4,4,4,128]{3,2,1,0:T(4,128)S(1)} %get-tuple-element.64, ...), kind=kLoop, calls=%fused_computation.64 | loop fusion | flops 31432704 | bytes 688128 | tf_op jit(solution)/shard_map/reduce_sum | solution.py:65
  319.7 15.0 %fusion.30 = (f32[4,4,4,128]{3,2,1,0:T(4,128)S(1)}, f32[4,4,4,128]{3,2,1,0:T(4,128)S(1)}, f32[4,4,4,128]{3,2,1,0:T(4,128)S(1)}) fusion(f32[4,4,4,128]{3,2,1,0:T(4,128)S(1)} %get-tuple-element.67, f32[4,4,4,128]{3,2,1,0:T(4,128)S(1)} %get-tuple-element.104, f32[4,4,4,128]{3,2,1,0:T(4,128)S(1)} %get-tuple-element.73, ...), kind=kLoop, calls=%fused_computation.70 | loop fusion | flops 31432704 | bytes 688128 | tf_op jit(solution)/shard_map/reduce_sum | solution.py:65
  334.8 15.1 %fusion.36 = (f32[4,4,4,128]{3,2,1,0:T(4,128)S(1)}, f32[4,4,4,128]{3,2,1,0:T(4,128)S(1)}, f32[4,4,4,128]{3,2,1,0:T(4,128)S(1)}) fusion(f32[4,4,4,128]{3,2,1,0:T(4,128)S(1)} %get-tuple-element.134, f32[4,4,4,128]{3,2,1,0:T(4,128)S(1)} %get-tuple-element.104, f32[4,4,4,128]{3,2,1,0:T(4,128)S(1)} %get-tuple-element.136, ...), kind=kLoop, calls=%fused_computation.76 | loop fusion | flops 31432704 | bytes 688128 | tf_op jit(solution)/shard_map/reduce_sum | solution.py:65
  349.9 18.9 %fusion.5 = (f32[4,4,4,128]{3,2,1,0:T(4,128)S(1)}, f32[4,4,4,128]{3,2,1,0:T(4,128)S(1)}, f32[4,4,4,128]{3,2,1,0:T(4,128)S(1)}, f32[4,4,4,128]{3,2,1,0:T(4,128)S(...) fusion(f32[4,4,4,128]{3,2,1,0:T(4,128)S(1)} %get-tuple-element.104, ...), kind=kLoop, calls=%fused_computation.45 | loop fusion | flops 61816832 | bytes 786432 | tf_op jit(solution)/shard_map/reduce_sum | solution.py:65
  369.5 5.1 copy.35
  374.6 89.8 %scatter_custom_fusion = f32[8192,3]{1,0:T(8,128)} fusion(s32[16384]{0:T(1024)} %bitcast.248, f32[16384,3]{1,0:T(8,128)} %copy.35, f32[]{:T(128)} %constant.77.clone.1), kind=kCustom, calls=%fused_computation.98 | custom fusion | flops 49152 | bytes 98816 | tf_op jit(solution)/shard_map/scatter-add | solution.py:182
  464.4 6.1 %bitcast_add_fusion = (f32[3,8192]{0,1:T(8,128)}, f32[3,8192]{0,1:T(8,128)}) fusion(f32[3,1,1,1,8192]{0,4,3,2,1:T(8,128)} %copy.31, f32[8192,3]{1,0:T(8,128)} %scatter_custom_fusion, f32[8192]{0:T(1024)S(1)} %bitcast.217), kind=kLoop, calls=%fused_computation.84 | loop fusion | flops 73728 | bytes 425984 | tf_op jit(solution)/shard_map/add | solution.py:184
  470.4 2.8 copy.36
  473.3 2.9 copy.37
  476.2 5.7 %collective-permute-start.6 = (f32[6,512]{1,0:T(8,128)S(1)}, f32[6,512]{1,0:T(8,128)S(1)}, u32[]{:S(2)}, u32[]{:S(2)}) collective-permute-start(f32[6,512]{1,0:T(8,128)S(1)} %get-tuple-element.98), channel_id=1, source_target_pairs={{0,16},{16,32},{32,48},{48,64},{64,80},{80,96},{96,112},{112,128},... | collective-permute-start | bytes 36872 | tf_op jit(solution)/shard_map/ppermute | solution.py:40
  481.8 1.9 collective-permute-start.7
  483.8 9.1 %collective-permute-done.7 = f32[6,512]{1,0:T(8,128)S(1)} collective-permute-done((f32[6,512]{1,0:T(8,128)S(1)}, f32[6,512]{1,0:T(8,128)S(1)}, u32[]{:S(2)}, u32[]{:S(2)}) %collective-permute-start.7) | collective-permute-done | bytes 12320 | tf_op jit(solution)/shard_map/ppermute | solution.py:40
  493.0 2.9 copy.38
  495.8 33.3 %gather_fusion = f32[9216,6]{1,0:T(8,128)} fusion(f32[6,9216]{0,1:T(8,128)} %copy.38, s32[9216]{0:T(1024)S(1)} %broadcast_clamp_fusion), kind=kCustom, calls=%fused_computation | custom fusion | bytes 479232 | tf_op jit(solution)/shard_map/jit(_take)/gather | solution.py:208
  529.1 11.3 %fusion = f32[6,1,1,1,9216]{0,4,3,2,1:T(8,128)} fusion(f32[9216,6]{1,0:T(8,128)} %gather_fusion, pred[9216]{0:T(1024)(128)(4,1)S(1)} %compare_and_fusion, pred[9216]{0:T(1024)(128)(4,1)S(1)} %iota_compare_fusion.4), kind=kLoop, calls=%fused_computation.40 | loop fusion | flops 110592 | bytes 460800 | tf_op jit(solution)/shard_map/jit(_where)/select_n | solution.py:208
  540.5 4.5 copy.39
  (68 shorter events, 6.3 us)
Async XLA Ops:
  6.5 25.3 %copy-start.4 = (s32[2,16,4,4]{1,3,2,0:T(4,128)S(1)}, s32[2,16,4,4]{1,3,2,0:T(4,128)}, u32[]{:S(2)}) copy-start(s32[2,16,4,4]{1,3,2,0:T(4,128)} %param.17) | copy-start | bytes 6148
  6.5 30.1 %copy-start.2 = (f32[3,1,1,1,8192]{4,3,2,1,0:T(1,128)S(1)}, f32[3,1,1,1,8192]{4,3,2,1,0:T(1,128)}, u32[]{:S(2)}) copy-start(f32[3,1,1,1,8192]{4,3,2,1,0:T(1,128)} %param.14) | copy-start | bytes 294916
  6.5 253.4 %all-reduce.6.cloned.1.call-start = ((), (), s32[]{:S(2)}) async-start(), calls=%async_computation | async-start | bytes 196608 | tf_op jit(solution)/shard_map/psum | solution.py:152
  10.2 249.7 %copy-start.5 = (f32[3,3]{1,0:T(4,128)S(1)}, f32[3,3]{1,0:T(4,128)}, u32[]{:S(2)}) copy-start(f32[3,3]{1,0:T(4,128)} %param.16) | copy-start | bytes 112
  13.3 258.6 %collective-permute-start = (f32[9,1,4,4,128]{4,3,2,1,0:T(4,128)S(1)}, f32[9,1,4,4,128]{4,3,2,1,0:T(4,128)S(1)}, u32[]{:S(2)}, u32[]{:S(2)}) collective-permute-start(f32[9,1,4,4,128]{4,3,2,1,0:T(4,128)S(1)} %get-tuple-element.97), channel_id=1, source_target_pairs={{16,0},{32,16},{48,32},{64,48},{80,64},{96,80},{112,96},{128,112},... | collective-permute-start | bytes 221192 | tf_op jit(solution)/shard_map/ppermute | solution.py:26
  15.9 256.1 %collective-permute-start.1 = (f32[9,1,4,4,128]{4,3,2,1,0:T(4,128)S(1)}, f32[9,1,4,4,128]{4,3,2,1,0:T(4,128)S(1)}, u32[]{:S(2)}, u32[]{:S(2)}) collective-permute-start(f32[9,1,4,4,128]{4,3,2,1,0:T(4,128)S(1)} %get-tuple-element.96), channel_id=1, source_target_pairs={{0,16},{16,32},{32,48},{48,64},{64,80},{80,96},{96,112},{112,128},... | collective-permute-start | bytes 221192 | tf_op jit(solution)/shard_map/ppermute | solution.py:25
  24.9 243.4 %collective-permute-start.2 = (f32[9,4,1,4,128]{4,3,2,1,0:T(4,128)S(1)}, f32[9,4,1,4,128]{4,3,2,1,0:T(4,128)S(1)}, u32[]{:S(2)}, u32[]{:S(2)}) collective-permute-start(f32[9,4,1,4,128]{4,3,2,1,0:T(4,128)S(1)} %get-tuple-element.95), channel_id=1, source_target_pairs={{4,0},{8,4},{12,8},{5,1},{9,5},{13,9},{6,2},{10,6},{14,10},{7,3},{... | collective-permute-start | bytes 221192 | tf_op jit(solution)/shard_map/ppermute | solution.py:26
  26.2 245.7 %collective-permute-start.3 = (f32[9,4,1,4,128]{4,3,2,1,0:T(4,128)S(1)}, f32[9,4,1,4,128]{4,3,2,1,0:T(4,128)S(1)}, u32[]{:S(2)}, u32[]{:S(2)}) collective-permute-start(f32[9,4,1,4,128]{4,3,2,1,0:T(4,128)S(1)} %get-tuple-element.94), channel_id=1, source_target_pairs={{0,4},{4,8},{8,12},{1,5},{5,9},{9,13},{2,6},{6,10},{10,14},{3,7},{... | collective-permute-start | bytes 221192 | tf_op jit(solution)/shard_map/ppermute | solution.py:25
  30.5 241.4 %collective-permute-start.4 = (f32[9,4,4,1,128]{4,3,2,1,0:T(1,128)S(1)}, f32[9,4,4,1,128]{4,3,2,1,0:T(1,128)S(1)}, u32[]{:S(2)}, u32[]{:S(2)}) collective-permute-start(f32[9,4,4,1,128]{4,3,2,1,0:T(1,128)S(1)} %get-tuple-element.92), channel_id=1, source_target_pairs={{1,0},{2,1},{3,2},{5,4},{6,5},{7,6},{9,8},{10,9},{11,10},{13,12},{... | collective-permute-start | bytes 221192 | tf_op jit(solution)/shard_map/ppermute | solution.py:26
  36.7 236.6 %copy-start = (f32[3,4,4,4,128]{4,3,2,1,0:T(4,128)S(1)}, f32[3,4,4,4,128]{4,3,2,1,0:T(4,128)}, u32[]{:S(2)}) copy-start(f32[3,4,4,4,128]{4,3,2,1,0:T(4,128)} %param.11) | copy-start | bytes 294916
  36.7 236.5 %copy-start.1 = (f32[3,4,4,4,128]{4,3,2,1,0:T(4,128)S(1)}, f32[3,4,4,4,128]{4,3,2,1,0:T(4,128)}, u32[]{:S(2)}) copy-start(f32[3,4,4,4,128]{4,3,2,1,0:T(4,128)} %param.9) | copy-start | bytes 294916
  268.3 4.9 collective-permute-start.5
  374.6 89.8 %copy-start.3 = (f32[1,1,1,8192]{3,2,1,0:T(1,128)S(1)}, f32[1,1,1,8192]{3,2,1,0:T(1,128)}, u32[]{:S(2)}) copy-start(f32[1,1,1,8192]{3,2,1,0:T(1,128)} %param.15) | copy-start | bytes 98308
  476.2 7.6 %collective-permute-start.6 = (f32[6,512]{1,0:T(8,128)S(1)}, f32[6,512]{1,0:T(8,128)S(1)}, u32[]{:S(2)}, u32[]{:S(2)}) collective-permute-start(f32[6,512]{1,0:T(8,128)S(1)} %get-tuple-element.98), channel_id=1, source_target_pairs={{0,16},{16,32},{32,48},{48,64},{64,80},{80,96},{96,112},{112,128},... | collective-permute-start | bytes 36872 | tf_op jit(solution)/shard_map/ppermute | solution.py:40
  481.8 11.1 %collective-permute-start.7 = (f32[6,512]{1,0:T(8,128)S(1)}, f32[6,512]{1,0:T(8,128)S(1)}, u32[]{:S(2)}, u32[]{:S(2)}) collective-permute-start(f32[6,512]{1,0:T(8,128)S(1)} %get-tuple-element.99), channel_id=1, source_target_pairs={{16,0},{32,16},{48,32},{64,48},{80,64},{96,80},{112,96},{128,112},... | collective-permute-start | bytes 36872 | tf_op jit(solution)/shard_map/ppermute | solution.py:40
Sparse Core Ops, SparseCore 0:
  12.9 247.0 all-reduce.5
where the time goes:
time: 553 us; the launch traced here: 552 us
  waiting for transfers between devices  230 us (42%)
  other arithmetic  206 us (37%)
  local copies, waits for them, and re-layouts  58.6 us (11%)
  starting transfers between devices  29.4 us (5%)
  between operations  17.1 us (3%)
  matrix products  9.9 us (2%)
    psum x1, waiting for transfers between devices, shards(): whole = lax.psum(whole, ('gx', 'gy', 'gz'))  220 us
    reduce_sum x6, other arithmetic, pair_term(): jnp.sum(weight * deltas[axis_id], axis=-1)  94.2 us
    scatter-add x1, other arithmetic, shards(): jax.ops.segment_sum(values, connect.reshape(-1), num_segments=nodes)  89.8 us
    gather x1, local copies, waits for them, and re-layouts, shards(): result = jnp.where(live[None], jnp.take(sectioning, source, axis=1), 0.0)  33.3 us
    ppermute x3, starting transfers between devices, extended(): lax.ppermute(last, axis, up)  16.6 us
    select_n x2, other arithmetic, shards(): result = jnp.where(live[None], jnp.take(sectioning, source, axis=1), 0.0)  11.5 us
  transfers between devices with their start and end apart: 9, of which 3 were waited for; matrix products, arithmetic and copies ran while one was open for 3% of the time, Pallas kernels for 0%

commit v1 on v0

v1 whole, which is shorter than its diff:
```python
import functools
import jax
import jax.numpy as jnp
from jax import lax
from jax.experimental import pallas as pl
from jax.experimental.pallas import tpu as pltpu
from jax.sharding import PartitionSpec as P

SOFTEN_NEAR = 0.25
SOFTEN_FAR = 4.0
NEAR_SCALE = 0.0625
FAR_SCALE = 0.03125
TIME_STEP = 0.1
AXES = ("gx", "gy", "gz")
F32 = jnp.float32
BF16 = jnp.bfloat16
LANES = 128
CELLS = 64
FACE = 16
SOURCES = CELLS + 6 * FACE
FACES = ("xlo", "xhi", "ylo", "yhi", "zlo", "zhi")
VMEM = 60 << 20


def face_rows(name):
    return {
        "xlo": [(0, 16, 1)],
        "xhi": [(48, 16, 1)],
        "ylo": [(16 * x, 4, 1) for x in range(4)],
        "yhi": [(16 * x + 12, 4, 1) for x in range(4)],
        "zlo": [(0, 16, 4)],
        "zhi": [(3, 16, 4)],
    }[name]


def split3(value):
    high = value.astype(BF16).astype(F32)
    rest = value - high
    middle = rest.astype(BF16).astype(F32)
    return high, middle, rest - middle


def prepare_kernel(offsets, burgers, lines, counts, masked, moments, *faces):
    slot = lax.broadcasted_iota(jnp.int32, (8, LANES), 1)
    row = lax.broadcasted_iota(jnp.int32, (8, LANES), 0)
    for group in range(8):
        live = jnp.zeros((8, LANES), jnp.int32)
        for s in range(8):
            cell = 8 * group + s
            live = jnp.where(row == s, counts[cell // 16, (cell // 4) % 4, cell % 4], live)
        for axis in range(3):
            block = burgers[axis, pl.ds(8 * group, 8), :]
            masked[axis, pl.ds(8 * group, 8), :] = jnp.where(slot < live, block, 0.0)
    for name, face in zip(FACES, faces):
        to = 0
        for start, size, stride in face_rows(name):
            at = pl.ds(start, size, stride=stride) if stride > 1 else pl.ds(start, size)
            for axis in range(3):
                face[axis, pl.ds(to, size), :] = offsets[axis, at, :]
                face[3 + axis, pl.ds(to, size), :] = masked[axis, at, :]
                face[6 + axis, pl.ds(to, size), :] = lines[axis, at, :]
            to += size
    rows = []
    for coarse in range(4):
        big_x, big_y = coarse // 2, coarse % 2
        groups = (4 * big_x + big_y, 4 * big_x + 2 + big_y)
        for a in range(3):
            for b in range(3):
                rows.append(
                    sum(
                        masked[a, pl.ds(8 * g, 8), :] * lines[b, pl.ds(8 * g, 8), :]
                        for g in groups
                    )
                )
    stack = jnp.concatenate(rows, axis=0)
    ones = jnp.ones((8, LANES), F32)
    summed = lax.dot_general(
        ones,
        stack,
        (((1,), (1,)), ((), ())),
        precision=lax.Precision.HIGHEST,
        preferred_element_type=F32,
    )
    n = lax.broadcasted_iota(jnp.int32, (288, LANES), 0)
    lane = lax.broadcasted_iota(jnp.int32, (288, LANES), 1)
    target = ((n // 72) * 2 + (n % 4) // 2) * 16 + (n // 8) % 9
    pick = (lane == target).astype(F32)
    packed = jnp.dot(summed, pick, precision=lax.Precision.HIGHEST, preferred_element_type=F32)
    moments[...] = jnp.broadcast_to(packed[0:1], moments.shape)


def source_index(target):
    x, y, z = target >> 4, (target >> 2) & 3, target & 3
    first = CELLS
    return [
        target,
        jnp.where(x > 0, target - 16, first + (target & 15)),
        jnp.where(x < 3, target + 16, first + 16 + (target & 15)),
        jnp.where(y > 0, target - 4, first + 32 + x * 4 + z),
        jnp.where(y < 3, target + 4, first + 48 + x * 4 + z),
        jnp.where(z > 0, target - 1, first + 64 + (target >> 2)),
        jnp.where(z < 3, target + 1, first + 80 + (target >> 2)),
    ]


PAIRS = ((0, 0), (0, 1), (1, 0), (0, 2), (2, 0), (1, 1))


def near_kernel(*refs):
    offsets, masked, lines = refs[:3]
    faces = refs[3:9]
    near = refs[9]
    rows_s, rows_t, source, target, points = refs[10:]
    blocks = []
    for first in range(0, CELLS, 16):
        cell = first + lax.broadcasted_iota(jnp.int32, (16, LANES), 0)
        corner = (cell // 16, (cell // 4) % 4, cell % 4)
        blocks.append(
            (
                first,
                [offsets[a, pl.ds(first, 16), :] + (corner[a].astype(F32) - 2.0) for a in range(3)],
                [masked[a, pl.ds(first, 16), :] for a in range(3)],
                [lines[a, pl.ds(first, 16), :] for a in range(3)],
            )
        )
    cell = lax.broadcasted_iota(jnp.int32, (16, LANES), 0)
    for f, face in enumerate(faces):
        fixed = f // 2
        others = [a for a in range(3) if a != fixed]
        corner = [None] * 3
        corner[fixed] = -3.0 if f % 2 == 0 else 2.0
        corner[others[0]] = (cell // 4).astype(F32) - 2.0
        corner[others[1]] = (cell % 4).astype(F32) - 2.0
        blocks.append(
            (
                CELLS + FACE * f,
                [face[a] + corner[a] for a in range(3)],
                [face[3 + a] for a in range(3)],
                [face[6 + a] for a in range(3)],
            )
        )
    one = jnp.ones((16, LANES), F32)
    zero = jnp.zeros((16, LANES), F32)
    rows_s[:, pl.ds(80, 48), :] = jnp.zeros((SOURCES, 48, LANES), F32)
    rows_t[:, pl.ds(80, 48), :] = jnp.zeros((CELLS, 48, LANES), F32)
    for first, place, burger, line in blocks:
        own = first < CELLS
        place_parts = [split3(p) for p in place]
        norm = split3(place[0] * place[0] + place[1] * place[1] + place[2] * place[2])
        outer = [split3(burger[a] * line[b]) for a in range(3) for b in range(3)]
        k = 0
        for s, t in PAIRS:
            for a in range(3):
                rows_s[pl.ds(first, 16), k, :] = place_parts[a][s]
                if own:
                    rows_t[pl.ds(first, 16), k, :] = -2.0 * place_parts[a][t]
                k += 1
        if own:
            shifted = split3(
                place[0] * place[0] + place[1] * place[1] + place[2] * place[2] + SOFTEN_NEAR
            )
        for s in range(3):
            rows_s[pl.ds(first, 16), k, :] = norm[s]
            if own:
                rows_t[pl.ds(first, 16), k, :] = one
            k += 1
        for s in range(3):
            rows_s[pl.ds(first, 16), k, :] = one
            if own:
                rows_t[pl.ds(first, 16), k, :] = shifted[s]
            k += 1
        for s, t in PAIRS:
            for ab in range(9):
                rows_s[pl.ds(first, 16), k, :] = outer[ab][s]
                if own:
                    rows_t[pl.ds(first, 16), k, :] = outer[ab][t]
                k += 1
        for k in (78, 79):
            rows_s[pl.ds(first, 16), k, :] = zero
            if own:
                rows_t[pl.ds(first, 16), k, :] = zero

    def arrange(c, carry):
        block = rows_s[c]
        source[c] = block.T.astype(BF16)
        head = block[0:24]
        points[c] = jnp.concatenate(
            [head[0:3], head[6:9], head[12:15], head[21:22], jnp.zeros((6, LANES), F32)], axis=0
        ).astype(BF16)
        return carry

    lax.fori_loop(0, SOURCES, arrange, 0)

    def arrange_target(c, carry):
        block = rows_t[c]
        row = lax.broadcasted_iota(jnp.int32, (LANES, LANES), 0)
        target[c, :, :LANES] = jnp.where(row < 24, block, 0.0).astype(BF16)
        target[c, :, LANES:] = jnp.where(row < 24, 0.0, block).astype(BF16)
        return carry

    lax.fori_loop(0, CELLS, arrange_target, 0)
    together = 2

    def step(i, carry):
        cells = [i * together + u for u in range(together)]
        sources = [source_index(c) for c in cells]
        stationary = [target[c] for c in cells]
        weights = [[] for _ in cells]
        spots = [[] for _ in cells]
        for k in range(7):
            for u in range(together):
                pair = jnp.dot(source[sources[u][k]], stationary[u], preferred_element_type=F32)
                inverse = lax.rsqrt(pair[:, :LANES])
                weight = pair[:, LANES:] * (inverse * inverse * inverse)
                high = weight.astype(BF16)
                low = (weight - high.astype(F32)).astype(BF16)
                weights[u].append(jnp.concatenate([high, low], axis=1))
                spots[u].append(points[sources[u][k]])
        for u in range(together):
            both = jnp.dot(
                jnp.concatenate(spots[u], axis=1),
                jnp.concatenate(weights[u], axis=0),
                preferred_element_type=F32,
            )
            sums = both[:, :LANES] + both[:, LANES:]
            moved = sums[0:3] + sums[3:6] + sums[6:9]
            total = sums[9:10]
            base = rows_t[cells[u], 0:24, :]
            place = -0.5 * (base[0:3] + base[3:6] + base[9:12])
            near[cells[u]] = place * total - moved
        return carry

    lax.fori_loop(0, CELLS // together, step, 0)


def node_kernel(
    gathered, near, masked, lines, stress, connect, node_pos, drag, fields, tail, head,
    values, sums, left, right,
):
    index_x, index_y, index_z = (lax.axis_index(a) for a in AXES)
    device = lax.broadcasted_iota(jnp.int32, (CELLS, 256), 1)
    cell = lax.broadcasted_iota(jnp.int32, (CELLS, 256), 0)
    gap = [
        (4 * index_x + cell // 16 - 4 * (device // 16)).astype(F32) - 0.5,
        (4 * index_y + (cell // 4) % 4 - 4 * ((device // 4) % 4)).astype(F32) - 0.5,
        (4 * index_z + cell % 4 - 4 * (device % 4)).astype(F32) - 0.5,
    ]
    square = [[gap[a] * gap[a], (gap[a] - 2.0) * (gap[a] - 2.0)] for a in range(3)]
    moments = gathered[...]
    lane = lax.broadcasted_iota(jnp.int32, (CELLS, LANES), 1)
    sigma = jnp.zeros((CELLS, LANES), F32)
    for sub in range(8):
        big_x, big_y, big_z = sub // 4, (sub // 2) % 2, sub % 2
        weight = lax.rsqrt(square[0][big_x] + square[1][big_y] + square[2][big_z] + SOFTEN_FAR)
        part = jnp.dot(
            weight, moments, precision=lax.Precision.HIGHEST, preferred_element_type=F32
        )
        sigma = jnp.where(lane // 16 == sub, part, sigma)
    for shift in (64, 32, 16):
        sigma = sigma + pltpu.roll(sigma, shift, 1)
    pull = [
        [FAR_SCALE * sigma[:, 3 * a + b : 3 * a + b + 1] + stress[a, b] for b in range(3)]
        for a in range(3)
    ]
    burger = [masked[a] for a in range(3)]
    line = [lines[a] for a in range(3)]
    pulled = [
        pull[a][0] * burger[0] + pull[a][1] * burger[1] + pull[a][2] * burger[2] for a in range(3)
    ]
    for a in range(3):
        b, c = (a + 1) % 3, (a + 2) % 3
        force = NEAR_SCALE * near[:, a, :] + (pulled[b] * line[c] - pulled[c] * line[b])
        parts = split3(0.5 * force)
        for p in range(3):
            values[3 * p + a] = parts[p]
    sums[...] = jnp.zeros(sums.shape, F32)
    rows_high = lax.broadcasted_iota(jnp.int32, (32, LANES), 0)
    rows_low = lax.broadcasted_iota(jnp.int32, (256, LANES), 0)
    step_cells = 4

    def scatter(i, carry):
        for u in range(step_cells):
            at = i * step_cells + u
            for end in range(2):
                column = (2 * u + end) * LANES
                node = connect[end, pl.ds(at, 1), :]
                chosen = rows_high == (node >> 8)
                for q in range(9):
                    left[pl.ds(32 * q, 32), pl.ds(column, LANES)] = jnp.where(
                        chosen, values[q, pl.ds(at, 1), :], 0.0
                    ).astype(BF16)
                right[:, pl.ds(column, LANES)] = (
                    (rows_low == (node & 255)).astype(F32).astype(BF16)
                )
        sums[...] += lax.dot_general(
            left[...], right[...], (((1,), (1,)), ((), ())), preferred_element_type=F32
        )
        return carry

    lax.fori_loop(0, CELLS // step_cells, scatter, 0)
    for a in range(3):
        force = (
            sums[pl.ds(32 * a, 32), :]
            + sums[pl.ds(96 + 32 * a, 32), :]
            + sums[pl.ds(192 + 32 * a, 32), :]
        )
        fields[3 + a, pl.ds(0, 32, stride=2), :] = force[:, :LANES]
        fields[3 + a, pl.ds(1, 32, stride=2), :] = force[:, LANES:]
    for a in range(3):
        velocity = fields[3 + a] / drag[...]
        fields[3 + a] = velocity
        fields[a] = node_pos[a] + TIME_STEP * velocity
    for a in range(6):
        tail[a] = fields[a, pl.ds(60, 4), :]
        head[a] = fields[a, pl.ds(0, 4), :]


def migrate_kernel(fields, below, above, shifts, out, joined):
    index_x, index_y, index_z = (lax.axis_index(a) for a in AXES)
    last = lax.axis_size("gx") - 1
    up_own = shifts[0, index_y, index_z, index_x]
    down_own = shifts[1, index_y, index_z, index_x]
    up_prev = jnp.where(
        index_x > 0, shifts[0, index_y, index_z, jnp.maximum(index_x - 1, 0)], 0
    )
    down_next = jnp.where(
        index_x < last, shifts[1, index_y, index_z, jnp.minimum(index_x + 1, last)], 0
    )
    kept = 8192 - up_own - down_own
    row = lax.broadcasted_iota(jnp.int32, (72, LANES), 0)
    lane = lax.broadcasted_iota(jnp.int32, (72, LANES), 1)
    position = row * LANES + lane
    pieces = (
        (512 - up_prev, position < up_prev),
        (512 + down_own - up_prev, position < up_prev + kept),
        (8704 - up_prev - kept, position < up_prev + kept + down_next),
    )
    for a in range(6):
        joined[pl.ds(0, 4), :] = below[a]
        joined[pl.ds(4, 64), :] = fields[a]
        joined[pl.ds(68, 4), :] = above[a]
        result = jnp.zeros((72, LANES), F32)
        for delta, within in reversed(pieces):
            rows, lanes = delta >> 7, delta & 127
            first = pltpu.roll(joined[pl.ds(rows, 72), :], (LANES - lanes) & 127, 1)
            second = pltpu.roll(joined[pl.ds(rows + 1, 72), :], (LANES - lanes) & 127, 1)
            moved = jnp.where(lane < LANES - lanes, first, second)
            result = jnp.where(within, moved, result)
        out[a] = result


def passed_along(array, axis, by):
    count = lax.axis_size(axis)
    pairs = [(i, i + by) for i in range(count) if 0 <= i + by < count]
    return lax.ppermute(array, axis, pairs)


def shape(*dims, dtype=F32):
    return jax.ShapeDtypeStruct(dims, dtype)


def shards(offsets, burgers, lines, counts, connect, node_pos, drag, stress, shifts):
    offsets = offsets.reshape(3, CELLS, LANES)
    burgers = burgers.reshape(3, CELLS, LANES)
    lines = lines.reshape(3, CELLS, LANES)
    connect = connect.reshape(2, CELLS, LANES)
    node_pos = node_pos.reshape(3, 64, LANES)
    drag = drag.reshape(64, LANES)
    shifts = shifts.transpose(0, 2, 3, 1)
    vmem = pl.BlockSpec(memory_space=pltpu.VMEM)
    smem = pl.BlockSpec(memory_space=pltpu.SMEM)
    params = pltpu.CompilerParams(vmem_limit_bytes=VMEM)
    masked, moments, *faces = pl.pallas_call(
        prepare_kernel,
        in_specs=[vmem, vmem, vmem, smem],
        out_shape=[shape(3, CELLS, LANES), shape(256, LANES)] + [shape(9, FACE, LANES)] * 6,
        compiler_params=params,
        name="prepare",
    )(offsets, burgers, lines, counts)
    by_name = dict(zip(FACES, faces))
    received = []
    for axis, name in zip(AXES, "xyz"):
        received.append(passed_along(by_name[name + "hi"], axis, 1))
        received.append(passed_along(by_name[name + "lo"], axis, -1))
    gathered = lax.all_to_all(
        moments.reshape(256, 1, LANES), AXES, 0, 0, tiled=True
    ).reshape(256, LANES)
    near = pl.pallas_call(
        near_kernel,
        in_specs=[vmem] * 9,
        out_shape=shape(CELLS, 3, LANES),
        scratch_shapes=[
            pltpu.VMEM((SOURCES, LANES, LANES), F32),
            pltpu.VMEM((CELLS, LANES, LANES), F32),
            pltpu.VMEM((SOURCES, LANES, LANES), BF16),
            pltpu.VMEM((CELLS, LANES, 2 * LANES), BF16),
            pltpu.VMEM((SOURCES, 16, LANES), BF16),
        ],
        compiler_params=params,
        name="near",
    )(offsets, masked, lines, *received)
    fields, tail, head = pl.pallas_call(
        node_kernel,
        in_specs=[vmem] * 4 + [smem] + [vmem] * 3,
        out_shape=[shape(6, 64, LANES), shape(6, 4, LANES), shape(6, 4, LANES)],
        scratch_shapes=[
            pltpu.VMEM((9, CELLS, LANES), F32),
            pltpu.VMEM((288, 256), F32),
            pltpu.VMEM((288, 1024), BF16),
            pltpu.VMEM((256, 1024), BF16),
        ],
        compiler_params=params,
        name="nodes",
    )(gathered, near, masked, lines, stress, connect, node_pos, drag)
    below = passed_along(tail, "gx", 1)
    above = passed_along(head, "gx", -1)
    out = pl.pallas_call(
        migrate_kernel,
        in_specs=[vmem] * 3 + [smem],
        out_shape=shape(6, 72, LANES),
        scratch_shapes=[pltpu.VMEM((96, LANES), F32)],
        compiler_params=params,
        name="migrate",
    )(fields, below, above, shifts)
    return out.reshape(6, 1, 1, 1, 72 * LANES)


def solution(mesh):
    cells = P(None, "gx", "gy", "gz", None)
    return jax.shard_map(
        shards,
        mesh=mesh,
        in_specs=(cells, cells, cells, P("gx", "gy", "gz"), cells, cells,
                  P("gx", "gy", "gz", None), P(), P()),
        out_specs=cells,
        check_vma=False,
    )
```

time: 553 us -> 119 us (0.22)
  waiting for transfers between devices: 230 us -> 13.1 us
  other arithmetic: 206 us -> 0 us
  local copies, waits for them, and re-layouts: 58.6 us -> 1.88 us
  Pallas kernels: 0 us -> 56.7 us
  between operations: 17.1 us -> 0.2 us
  starting transfers between devices: 29.4 us -> 46.2 us
  matrix products: 9.9 us -> 0 us
    psum x1 -> x0, waiting for transfers between devices: 220 us -> none  [shards(): whole = lax.psum(whole, ('gx', 'gy', 'gz'))]
    reduce_sum x7 -> x0, other arithmetic: 94.3 us -> none  [the longest x6 94.2 us: pair_term(): jnp.sum(weight * deltas[axis_id], axis=-1)]
    scatter-add x1 -> x0, other arithmetic: 89.8 us -> none  [shards(): jax.ops.segment_sum(values, connect.reshape(-1), num_segments=nodes)]
    pallas_call x0 -> x4, Pallas kernels: none -> 56.7 us  [the longest x1 41.3 us: shards(): pl.pallas_call(near_kernel, in_specs=[vmem] * 9, out_shape=shape(CELLS, 3...]
    gather x1 -> x0, local copies, waits for them, and re-layouts: 33.3 us -> none  [shards(): result = jnp.where(live[None], jnp.take(sectioning, source, axis=1), 0.0)]
    ppermute x2 -> x8, starting transfers between devices: 7.57 us -> 31.5 us  [passed_along(): return lax.ppermute(array, axis, pairs)]
    ppermute x6 -> x0, starting transfers between devices: 21.8 us -> none  [the longest x3 16.6 us: extended(): lax.ppermute(last, axis, up)]
    all_to_all x0 -> x1, starting transfers between devices: none -> 14.8 us  [shards(): lax.all_to_all(moments.reshape(256, 1, LANES), AXES, 0, 0, tiled=True)]
  transfers between devices with their start and end apart: 9 -> 9, of which waited for: 3 -> 3; matrix products, arithmetic and copies ran while one was open for 3% -> 0% of each run, Pallas kernels for 0% -> 35%
where the time goes in v1:
time: 119 us; the launch traced here: 118 us
  Pallas kernels  56.7 us (48%)
  starting transfers between devices  46.2 us (39%)
  waiting for transfers between devices  13.1 us (11%)
  local copies, waits for them, and re-layouts  1.88 us (2%)
    pallas_call x1, Pallas kernels, shards(): pl.pallas_call(near_kernel, in_specs=[vmem] * 9, out_shape=shape(CELLS, 3...  41.3 us
    ppermute x8, starting transfers between devices, passed_along(): return lax.ppermute(array, axis, pairs)  31.5 us
    all_to_all x1, starting transfers between devices, shards(): lax.all_to_all(moments.reshape(256, 1, LANES), AXES, 0, 0, tiled=True)  14.8 us
    ppermute x8, waiting for transfers between devices, passed_along(): return lax.ppermute(array, axis, pairs)  13.1 us
    pallas_call x1, Pallas kernels, shards(): pl.pallas_call(node_kernel, in_specs=[vmem] * 4 + [smem] + [vmem] * 3, ou...  11 us
  transfers between devices with their start and end apart: 9, of which 3 were waited for; matrix products, arithmetic and copies ran while one was open for 0% of the time, Pallas kernels for 35%

profile of v1, /device:TPU:25, one launch (start us, length us, event | category | flops | bytes accessed | tf_op | source)
XLA Modules:
  0.0 118.1 jit_solution(2668973468057086132)
XLA Ops:
  0.0 2.3 %prepare.1 = (f32[3,64,128]{2,1,0:T(8,128)}, f32[256,128]{1,0:T(8,128)}, f32[9,16,128]{2,1,0:T(8,128)}, f32[9,16,128]{2,1,0:T(8,128)}, f32[9,16,128]{2,1,0:T(8,1...) custom-call(f32[3,64,128]{2,1,0:T(8,128)} %bitcast.16, f32[3,64,128]{2,1,0:T(8,128)} %bitcast.20, ...), custom_call_target="tpu_custom_call" | custom-call | tf_op jit(solution)/shard_map/prepare/pallas_call | solution.py:373
  2.3 0.0 copy-start.10
  2.3 0.0 copy-start.9
  2.3 14.8 %all-to-all-start = ((f32[256,1,128]{2,1,0:T(1,128)}), f32[256,1,128]{2,1,0:T(1,128)S(1)}, u32[]{:S(2)}, u32[]{:S(2)}) async-start(f32[256,1,128]{2,1,0:T(1,128)} %bitcast.18), calls=%async_computation | async-start | bytes 262144 | tf_op jit(solution)/shard_map/all_to_all | solution.py:385
  17.0 8.1 %collective-permute-start = (f32[9,16,128]{2,1,0:T(8,128)}, f32[9,16,128]{2,1,0:T(8,128)S(1)}, u32[]{:S(2)}, u32[]{:S(2)}) collective-permute-start(f32[9,16,128]{2,1,0:T(8,128)} %get-tuple-element.18), channel_id=1, source_target_pairs={{0,16},{16,32},{32,48},{48,64},{64,80},{80,96},{96,112},{112,128},... | collective-permute-start | bytes 221192 | tf_op jit(solution)/shard_map/ppermute | solution.py:355
  25.2 1.9 %collective-permute-start.1 = (f32[9,16,128]{2,1,0:T(8,128)}, f32[9,16,128]{2,1,0:T(8,128)S(1)}, u32[]{:S(2)}, u32[]{:S(2)}) collective-permute-start(f32[9,16,128]{2,1,0:T(8,128)} %get-tuple-element.19), channel_id=1, source_target_pairs={{16,0},{32,16},{48,32},{64,48},{80,64},{96,80},{112,96},{128,112},... | collective-permute-start | bytes 221192 | tf_op jit(solution)/shard_map/ppermute | solution.py:355
  27.1 2.5 %collective-permute-start.2 = (f32[9,16,128]{2,1,0:T(8,128)}, f32[9,16,128]{2,1,0:T(8,128)S(1)}, u32[]{:S(2)}, u32[]{:S(2)}) collective-permute-start(f32[9,16,128]{2,1,0:T(8,128)} %get-tuple-element.20), channel_id=1, source_target_pairs={{0,4},{4,8},{8,12},{1,5},{5,9},{9,13},{2,6},{6,10},{10,14},{3,7},{... | collective-permute-start | bytes 221192 | tf_op jit(solution)/shard_map/ppermute | solution.py:355
  29.6 0.0 copy-done.11
  29.6 1.3 %collective-permute-start.3 = (f32[9,16,128]{2,1,0:T(8,128)S(1)}, f32[9,16,128]{2,1,0:T(8,128)S(1)}, u32[]{:S(2)}, u32[]{:S(2)}) collective-permute-start(f32[9,16,128]{2,1,0:T(8,128)S(1)} %copy-done.11), channel_id=1, source_target_pairs={{4,0},{8,4},{12,8},{5,1},{9,5},{13,9},{6,2},{10,6},{14,10},{7,3},{... | collective-permute-start | bytes 221192 | tf_op jit(solution)/shard_map/ppermute | solution.py:355
  30.9 0.0 copy-done.10
  30.9 3.1 %collective-permute-start.4 = (f32[9,16,128]{2,1,0:T(8,128)S(1)}, f32[9,16,128]{2,1,0:T(8,128)S(1)}, u32[]{:S(2)}, u32[]{:S(2)}) collective-permute-start(f32[9,16,128]{2,1,0:T(8,128)S(1)} %copy-done.10), channel_id=1, source_target_pairs={{0,1},{1,2},{2,3},{4,5},{5,6},{6,7},{8,9},{9,10},{10,11},{12,13},{... | collective-permute-start | bytes 221192 | tf_op jit(solution)/shard_map/ppermute | solution.py:355
  34.0 0.0 collective-permute-done.refs_3_
  34.0 0.0 copy-start.1
  34.0 0.0 copy-done.9
  34.0 1.3 %collective-permute-start.5 = (f32[9,16,128]{2,1,0:T(8,128)S(1)}, f32[9,16,128]{2,1,0:T(8,128)S(1)}, u32[]{:S(2)}, u32[]{:S(2)}) collective-permute-start(f32[9,16,128]{2,1,0:T(8,128)S(1)} %copy-done.9), channel_id=1, source_target_pairs={{1,0},{2,1},{3,2},{5,4},{6,5},{7,6},{9,8},{10,9},{11,10},{13,12},{... | collective-permute-start | bytes 221192 | tf_op jit(solution)/shard_map/ppermute | solution.py:355
  35.3 1.7 %collective-permute-done.1.refs_4_ = f32[9,16,128]{2,1,0:T(8,128)S(1)} collective-permute-done((f32[9,16,128]{2,1,0:T(8,128)}, f32[9,16,128]{2,1,0:T(8,128)S(1)}, u32[]{:S(2)}, u32[]{:S(2)}) %collective-permute-start.1) | collective-permute-done | bytes 73760 | tf_op jit(solution)/shard_map/ppermute | solution.py:355
  37.1 0.0 collective-permute-done.2.refs_5_
  37.1 0.0 collective-permute-done.3.refs_6_
  37.1 0.0 collective-permute-done.4.refs_7_
  37.1 2.0 %collective-permute-done.5.refs_8_ = f32[9,16,128]{2,1,0:T(8,128)S(1)} collective-permute-done((f32[9,16,128]{2,1,0:T(8,128)S(1)}, f32[9,16,128]{2,1,0:T(8,128)S(1)}, u32[]{:S(2)}, u32[]{:S(2)}) %collective-permute-start.5) | collective-permute-done | bytes 73760 | tf_op jit(solution)/shard_map/ppermute | solution.py:355
  39.1 0.0 copy-done.3
  39.2 0.6 copy-done.6
  39.8 41.3 %near.1 = f32[64,3,128]{2,1,0:T(4,128)} custom-call(f32[3,64,128]{2,1,0:T(8,128)} %bitcast.17, f32[3,64,128]{2,1,0:T(8,128)} %get-tuple-element.17.refs_1_.masked, f32[3,64,128]{2,1,0:T(8,128)} %bitcast.13, f32[9,16,128]{2,1,0:T(8,128)} %copy-done.1, f32[9,16,128]{2,1,0:T(8,128)} %copy-done.2, f32[9,16,128]{2,1,0:T(8,128)} %copy-done.3, ...), custom_call_target="tpu_custom_call" | custom-call | tf_op jit(solution)/shard_map/near/pallas_call | solution.py:388
  81.0 0.0 all-to-all-done
  81.0 0.7 copy-done
  81.7 11.0 %nodes.1 = (f32[6,64,128]{2,1,0:T(8,128)}, f32[6,4,128]{2,1,0:T(4,128)}, f32[6,4,128]{2,1,0:T(4,128)}) custom-call(f32[256,128]{1,0:T(8,128)} %bitcast.15, f32[64,3,128]{2,1,0:T(4,128)} %near.1, f32[3,64,128]{2,1,0:T(8,128)} %get-tuple-element.17.refs_1_.masked, f32[3,64,128]{2,1,0:T(8,128)} %bitcast.14, f32[3,3]{1,0:T(4,128)} %stress.1, ...), custom_call_target="tpu_custom_call" | custom-call | tf_op jit(solution)/shard_map/nodes/pallas_call | solution.py:402
  92.7 11.4 %collective-permute-start.6 = (f32[6,4,128]{2,1,0:T(4,128)}, f32[6,4,128]{2,1,0:T(4,128)S(1)}, u32[]{:S(2)}, u32[]{:S(2)}) collective-permute-start(f32[6,4,128]{2,1,0:T(4,128)} %get-tuple-element.25), channel_id=1, source_target_pairs={{0,16},{16,32},{32,48},{48,64},{64,80},{80,96},{96,112},{112,128},... | collective-permute-start | bytes 36872 | tf_op jit(solution)/shard_map/ppermute | solution.py:355
  104.1 1.9 %collective-permute-start.7 = (f32[6,4,128]{2,1,0:T(4,128)}, f32[6,4,128]{2,1,0:T(4,128)S(1)}, u32[]{:S(2)}, u32[]{:S(2)}) collective-permute-start(f32[6,4,128]{2,1,0:T(4,128)} %get-tuple-element.26), channel_id=1, source_target_pairs={{16,0},{32,16},{48,32},{64,48},{80,64},{96,80},{112,96},{128,112},... | collective-permute-start | bytes 36872 | tf_op jit(solution)/shard_map/ppermute | solution.py:355
  106.0 0.0 collective-permute-done.6.below
  106.0 9.3 %collective-permute-done.7.above = f32[6,4,128]{2,1,0:T(4,128)S(1)} collective-permute-done((f32[6,4,128]{2,1,0:T(4,128)}, f32[6,4,128]{2,1,0:T(4,128)S(1)}, u32[]{:S(2)}, u32[]{:S(2)}) %collective-permute-start.7) | collective-permute-done | bytes 12320 | tf_op jit(solution)/shard_map/ppermute | solution.py:355
  115.3 0.6 copy-done.8
  115.9 2.2 %migrate.1 = f32[6,72,128]{2,1,0:T(8,128)} custom-call(f32[6,64,128]{2,1,0:T(8,128)} %get-tuple-element.24.fields, f32[6,4,128]{2,1,0:T(4,128)} %copy-done.7, f32[6,4,128]{2,1,0:T(4,128)} %copy-done.8, s32[2,4,4,16]{3,2,1,0:T(4,128)} %bitcast.23), custom_call_target="tpu_custom_call" | custom-call | tf_op jit(solution)/shard_map/migrate/pallas_call | solution.py:417
  (14 shorter events, 0.0 us)
Async XLA Ops:
  2.3 27.3 %copy-start.11 = (f32[9,16,128]{2,1,0:T(8,128)S(1)}, f32[9,16,128]{2,1,0:T(8,128)}, u32[]{:S(2)}) copy-start(f32[9,16,128]{2,1,0:T(8,128)} %get-tuple-element.21) | copy-start | bytes 221188
  2.3 28.6 %copy-start.10 = (f32[9,16,128]{2,1,0:T(8,128)S(1)}, f32[9,16,128]{2,1,0:T(8,128)}, u32[]{:S(2)}) copy-start(f32[9,16,128]{2,1,0:T(8,128)} %get-tuple-element.22) | copy-start | bytes 221188
  2.3 31.8 %copy-start.9 = (f32[9,16,128]{2,1,0:T(8,128)S(1)}, f32[9,16,128]{2,1,0:T(8,128)}, u32[]{:S(2)}) copy-start(f32[9,16,128]{2,1,0:T(8,128)} %get-tuple-element.23) | copy-start | bytes 221188
  2.3 78.7 %all-to-all-start = ((f32[256,1,128]{2,1,0:T(1,128)}), f32[256,1,128]{2,1,0:T(1,128)S(1)}, u32[]{:S(2)}, u32[]{:S(2)}) async-start(f32[256,1,128]{2,1,0:T(1,128)} %bitcast.18), calls=%async_computation | async-start | bytes 262144 | tf_op jit(solution)/shard_map/all_to_all | solution.py:385
  17.0 17.0 %collective-permute-start = (f32[9,16,128]{2,1,0:T(8,128)}, f32[9,16,128]{2,1,0:T(8,128)S(1)}, u32[]{:S(2)}, u32[]{:S(2)}) collective-permute-start(f32[9,16,128]{2,1,0:T(8,128)} %get-tuple-element.18), channel_id=1, source_target_pairs={{0,16},{16,32},{32,48},{48,64},{64,80},{80,96},{96,112},{112,128},... | collective-permute-start | bytes 221192 | tf_op jit(solution)/shard_map/ppermute | solution.py:355
  25.2 11.9 %collective-permute-start.1 = (f32[9,16,128]{2,1,0:T(8,128)}, f32[9,16,128]{2,1,0:T(8,128)S(1)}, u32[]{:S(2)}, u32[]{:S(2)}) collective-permute-start(f32[9,16,128]{2,1,0:T(8,128)} %get-tuple-element.19), channel_id=1, source_target_pairs={{16,0},{32,16},{48,32},{64,48},{80,64},{96,80},{112,96},{128,112},... | collective-permute-start | bytes 221192 | tf_op jit(solution)/shard_map/ppermute | solution.py:355
  27.1 10.0 %collective-permute-start.2 = (f32[9,16,128]{2,1,0:T(8,128)}, f32[9,16,128]{2,1,0:T(8,128)S(1)}, u32[]{:S(2)}, u32[]{:S(2)}) collective-permute-start(f32[9,16,128]{2,1,0:T(8,128)} %get-tuple-element.20), channel_id=1, source_target_pairs={{0,4},{4,8},{8,12},{1,5},{5,9},{9,13},{2,6},{6,10},{10,14},{3,7},{... | collective-permute-start | bytes 221192 | tf_op jit(solution)/shard_map/ppermute | solution.py:355
  29.6 7.5 %collective-permute-start.3 = (f32[9,16,128]{2,1,0:T(8,128)S(1)}, f32[9,16,128]{2,1,0:T(8,128)S(1)}, u32[]{:S(2)}, u32[]{:S(2)}) collective-permute-start(f32[9,16,128]{2,1,0:T(8,128)S(1)} %copy-done.11), channel_id=1, source_target_pairs={{4,0},{8,4},{12,8},{5,1},{9,5},{13,9},{6,2},{10,6},{14,10},{7,3},{... | collective-permute-start | bytes 221192 | tf_op jit(solution)/shard_map/ppermute | solution.py:355
  30.9 6.2 %collective-permute-start.4 = (f32[9,16,128]{2,1,0:T(8,128)S(1)}, f32[9,16,128]{2,1,0:T(8,128)S(1)}, u32[]{:S(2)}, u32[]{:S(2)}) collective-permute-start(f32[9,16,128]{2,1,0:T(8,128)S(1)} %copy-done.10), channel_id=1, source_target_pairs={{0,1},{1,2},{2,3},{4,5},{5,6},{6,7},{8,9},{9,10},{10,11},{12,13},{... | collective-permute-start | bytes 221192 | tf_op jit(solution)/shard_map/ppermute | solution.py:355
  34.0 5.1 %copy-start.1 = (f32[9,16,128]{2,1,0:T(8,128)}, f32[9,16,128]{2,1,0:T(8,128)S(1)}, u32[]{:S(2)}) copy-start(f32[9,16,128]{2,1,0:T(8,128)S(1)} %collective-permute-done.refs_3_) | copy-start | bytes 221188
  34.0 5.1 %collective-permute-start.5 = (f32[9,16,128]{2,1,0:T(8,128)S(1)}, f32[9,16,128]{2,1,0:T(8,128)S(1)}, u32[]{:S(2)}, u32[]{:S(2)}) collective-permute-start(f32[9,16,128]{2,1,0:T(8,128)S(1)} %copy-done.9), channel_id=1, source_target_pairs={{1,0},{2,1},{3,2},{5,4},{6,5},{7,6},{9,8},{10,9},{11,10},{13,12},{... | collective-permute-start | bytes 221192 | tf_op jit(solution)/shard_map/ppermute | solution.py:355
  37.1 2.1 %copy-start.2 = (f32[9,16,128]{2,1,0:T(8,128)}, f32[9,16,128]{2,1,0:T(8,128)S(1)}, u32[]{:S(2)}) copy-start(f32[9,16,128]{2,1,0:T(8,128)S(1)} %collective-permute-done.1.refs_4_) | copy-start | bytes 221188
  37.1 2.1 %copy-start.3 = (f32[9,16,128]{2,1,0:T(8,128)}, f32[9,16,128]{2,1,0:T(8,128)S(1)}, u32[]{:S(2)}) copy-start(f32[9,16,128]{2,1,0:T(8,128)S(1)} %collective-permute-done.2.refs_5_) | copy-start | bytes 221188
  37.1 2.1 %copy-start.4 = (f32[9,16,128]{2,1,0:T(8,128)}, f32[9,16,128]{2,1,0:T(8,128)S(1)}, u32[]{:S(2)}) copy-start(f32[9,16,128]{2,1,0:T(8,128)S(1)} %collective-permute-done.3.refs_6_) | copy-start | bytes 221188
  37.1 2.1 %copy-start.5 = (f32[9,16,128]{2,1,0:T(8,128)}, f32[9,16,128]{2,1,0:T(8,128)S(1)}, u32[]{:S(2)}) copy-start(f32[9,16,128]{2,1,0:T(8,128)S(1)} %collective-permute-done.4.refs_7_) | copy-start | bytes 221188
  39.1 0.6 copy-start.6
  81.0 0.7 copy-start
  92.7 13.3 %collective-permute-start.6 = (f32[6,4,128]{2,1,0:T(4,128)}, f32[6,4,128]{2,1,0:T(4,128)S(1)}, u32[]{:S(2)}, u32[]{:S(2)}) collective-permute-start(f32[6,4,128]{2,1,0:T(4,128)} %get-tuple-element.25), channel_id=1, source_target_pairs={{0,16},{16,32},{32,48},{48,64},{64,80},{80,96},{96,112},{112,128},... | collective-permute-start | bytes 36872 | tf_op jit(solution)/shard_map/ppermute | solution.py:355
  104.1 11.2 %collective-permute-start.7 = (f32[6,4,128]{2,1,0:T(4,128)}, f32[6,4,128]{2,1,0:T(4,128)S(1)}, u32[]{:S(2)}, u32[]{:S(2)}) collective-permute-start(f32[6,4,128]{2,1,0:T(4,128)} %get-tuple-element.26), channel_id=1, source_target_pairs={{16,0},{32,16},{48,32},{64,48},{80,64},{96,80},{112,96},{128,112},... | collective-permute-start | bytes 36872 | tf_op jit(solution)/shard_map/ppermute | solution.py:355
  106.0 9.3 %copy-start.7 = (f32[6,4,128]{2,1,0:T(4,128)}, f32[6,4,128]{2,1,0:T(4,128)S(1)}, u32[]{:S(2)}) copy-start(f32[6,4,128]{2,1,0:T(4,128)S(1)} %collective-permute-done.6.below) | copy-start | bytes 36868
  115.3 0.6 copy-start.8

commit v2 on v1

--- a/solution.py
+++ b/solution.py
@@ -15,22 +15,19 @@
 F32 = jnp.float32
 BF16 = jnp.bfloat16
 LANES = 128
+DEPTH = 64
 CELLS = 64
 FACE = 16
 SOURCES = CELLS + 6 * FACE
-FACES = ("xlo", "xhi", "ylo", "yhi", "zlo", "zhi")
 VMEM = 60 << 20
 
 
-def face_rows(name):
-    return {
-        "xlo": [(0, 16, 1)],
-        "xhi": [(48, 16, 1)],
-        "ylo": [(16 * x, 4, 1) for x in range(4)],
-        "yhi": [(16 * x + 12, 4, 1) for x in range(4)],
-        "zlo": [(0, 16, 4)],
-        "zhi": [(3, 16, 4)],
-    }[name]
+def face_rows(axis):
+    return (
+        [(0, 48, 16, 1)],
+        [(16 * x, 16 * x + 12, 4, 1) for x in range(4)],
+        [(0, 3, 16, 4)],
+    )[axis]
 
 
 def split3(value):
@@ -40,7 +37,7 @@
     return high, middle, rest - middle
 
 
-def prepare_kernel(offsets, burgers, lines, counts, masked, moments, *faces):
+def prepare_kernel(offsets, burgers, lines, counts, masked, *sends):
     slot = lax.broadcasted_iota(jnp.int32, (8, LANES), 1)
     row = lax.broadcasted_iota(jnp.int32, (8, LANES), 0)
     for group in range(8):
@@ -51,15 +48,25 @@
         for axis in range(3):
             block = burgers[axis, pl.ds(8 * group, 8), :]
             masked[axis, pl.ds(8 * group, 8), :] = jnp.where(slot < live, block, 0.0)
-    for name, face in zip(FACES, faces):
+    for axis in range(3):
+        even = lax.axis_index(AXES[axis]) % 2 == 0
         to = 0
-        for start, size, stride in face_rows(name):
-            at = pl.ds(start, size, stride=stride) if stride > 1 else pl.ds(start, size)
-            for axis in range(3):
-                face[axis, pl.ds(to, size), :] = offsets[axis, at, :]
-                face[3 + axis, pl.ds(to, size), :] = masked[axis, at, :]
-                face[6 + axis, pl.ds(to, size), :] = lines[axis, at, :]
+        for low, high, size, stride in face_rows(axis):
+            at_low = pl.ds(low, size, stride=stride) if stride > 1 else pl.ds(low, size)
+            at_high = pl.ds(high, size, stride=stride) if stride > 1 else pl.ds(high, size)
+            for a in range(3):
+                for part, array in enumerate((offsets, masked, lines)):
+                    of_low, of_high = array[a, at_low, :], array[a, at_high, :]
+                    sends[2 * axis][3 * part + a, pl.ds(to, size), :] = jnp.where(
+                        even, of_high, of_low
+                    )
+                    sends[2 * axis + 1][3 * part + a, pl.ds(to, size), :] = jnp.where(
+                        even, of_low, of_high
+                    )
             to += size
+
+
+def moments_kernel(masked, lines, moments):
     rows = []
     for coarse in range(4):
         big_x, big_y = coarse // 2, coarse % 2
@@ -91,15 +98,17 @@
 
 def source_index(target):
     x, y, z = target >> 4, (target >> 2) & 3, target & 3
-    first = CELLS
+    odd = [lax.axis_index(a) & 1 for a in AXES]
+    upper = [CELLS + 2 * FACE * a + FACE * odd[a] for a in range(3)]
+    lower = [CELLS + 2 * FACE * a + FACE * (1 - odd[a]) for a in range(3)]
     return [
         target,
-        jnp.where(x > 0, target - 16, first + (target & 15)),
-        jnp.where(x < 3, target + 16, first + 16 + (target & 15)),
-        jnp.where(y > 0, target - 4, first + 32 + x * 4 + z),
-        jnp.where(y < 3, target + 4, first + 48 + x * 4 + z),
-        jnp.where(z > 0, target - 1, first + 64 + (target >> 2)),
-        jnp.where(z < 3, target + 1, first + 80 + (target >> 2)),
+        jnp.where(x > 0, target - 16, lower[0] + (target & 15)),
+        jnp.where(x < 3, target + 16, upper[0] + (target & 15)),
+        jnp.where(y > 0, target - 4, lower[1] + x * 4 + z),
+        jnp.where(y < 3, target + 4, upper[1] + x * 4 + z),
+        jnp.where(z > 0, target - 1, lower[2] + (target >> 2)),
+        jnp.where(z < 3, target + 1, upper[2] + (target >> 2)),
     ]
 
 
@@ -128,7 +137,8 @@
         fixed = f // 2
         others = [a for a in range(3) if a != fixed]
         corner = [None] * 3
-        corner[fixed] = -3.0 if f % 2 == 0 else 2.0
+        upper = lax.axis_index(AXES[fixed]) % 2 == f % 2
+        corner[fixed] = jnp.where(upper, 2.0, -3.0).astype(F32)
         corner[others[0]] = (cell // 4).astype(F32) - 2.0
         corner[others[1]] = (cell % 4).astype(F32) - 2.0
         blocks.append(
@@ -140,9 +150,8 @@
             )
         )
     one = jnp.ones((16, LANES), F32)
-    zero = jnp.zeros((16, LANES), F32)
-    rows_s[:, pl.ds(80, 48), :] = jnp.zeros((SOURCES, 48, LANES), F32)
-    rows_t[:, pl.ds(80, 48), :] = jnp.zeros((CELLS, 48, LANES), F32)
+    rows_s[:, pl.ds(48, DEPTH - 48), :] = jnp.zeros((SOURCES, DEPTH - 48, LANES), F32)
+    rows_t[:, pl.ds(48, DEPTH - 48), :] = jnp.zeros((CELLS, DEPTH - 48, LANES), F32)
     for first, place, burger, line in blocks:
         own = first < CELLS
         place_parts = [split3(p) for p in place]
@@ -169,36 +178,32 @@
             if own:
                 rows_t[pl.ds(first, 16), k, :] = shifted[s]
             k += 1
-        for s, t in PAIRS:
+        for s, t in PAIRS[:3]:
             for ab in range(9):
                 rows_s[pl.ds(first, 16), k, :] = outer[ab][s]
                 if own:
                     rows_t[pl.ds(first, 16), k, :] = outer[ab][t]
                 k += 1
-        for k in (78, 79):
-            rows_s[pl.ds(first, 16), k, :] = zero
-            if own:
-                rows_t[pl.ds(first, 16), k, :] = zero
 
     def arrange(c, carry):
         block = rows_s[c]
-        source[c] = block.T.astype(BF16)
+        source[c] = block.astype(BF16).T
         head = block[0:24]
         points[c] = jnp.concatenate(
             [head[0:3], head[6:9], head[12:15], head[21:22], jnp.zeros((6, LANES), F32)], axis=0
         ).astype(BF16)
         return carry
 
-    lax.fori_loop(0, SOURCES, arrange, 0)
+    lax.fori_loop(0, SOURCES, arrange, 0, unroll=8)
 
     def arrange_target(c, carry):
         block = rows_t[c]
-        row = lax.broadcasted_iota(jnp.int32, (LANES, LANES), 0)
+        row = lax.broadcasted_iota(jnp.int32, (DEPTH, LANES), 0)
         target[c, :, :LANES] = jnp.where(row < 24, block, 0.0).astype(BF16)
         target[c, :, LANES:] = jnp.where(row < 24, 0.0, block).astype(BF16)
         return carry
 
-    lax.fori_loop(0, CELLS, arrange_target, 0)
+    lax.fori_loop(0, CELLS, arrange_target, 0, unroll=4)
     together = 2
 
     def step(i, carry):
@@ -234,7 +239,7 @@
 
 
 def node_kernel(
-    gathered, near, masked, lines, stress, connect, node_pos, drag, fields, tail, head,
+    gathered, near, masked, lines, stress, connect, node_pos, drag, fields, first, second,
     values, sums, left, right,
 ):
     index_x, index_y, index_z = (lax.axis_index(a) for a in AXES)
@@ -310,14 +315,18 @@
         velocity = fields[3 + a] / drag[...]
         fields[3 + a] = velocity
         fields[a] = node_pos[a] + TIME_STEP * velocity
+    even = index_x % 2 == 0
     for a in range(6):
-        tail[a] = fields[a, pl.ds(60, 4), :]
-        head[a] = fields[a, pl.ds(0, 4), :]
-
-
-def migrate_kernel(fields, below, above, shifts, out, joined):
+        tail = fields[a, pl.ds(60, 4), :]
+        head = fields[a, pl.ds(0, 4), :]
+        first[a] = jnp.where(even, tail, head)
+        second[a] = jnp.where(even, head, tail)
+
+
+def migrate_kernel(fields, first, second, shifts, out, joined):
     index_x, index_y, index_z = (lax.axis_index(a) for a in AXES)
     last = lax.axis_size("gx") - 1
+    even = index_x % 2 == 0
     up_own = shifts[0, index_y, index_z, index_x]
     down_own = shifts[1, index_y, index_z, index_x]
     up_prev = jnp.where(
@@ -336,23 +345,22 @@
         (8704 - up_prev - kept, position < up_prev + kept + down_next),
     )
     for a in range(6):
-        joined[pl.ds(0, 4), :] = below[a]
+        joined[pl.ds(0, 4), :] = jnp.where(even, second[a], first[a])
         joined[pl.ds(4, 64), :] = fields[a]
-        joined[pl.ds(68, 4), :] = above[a]
+        joined[pl.ds(68, 4), :] = jnp.where(even, first[a], second[a])
         result = jnp.zeros((72, LANES), F32)
         for delta, within in reversed(pieces):
             rows, lanes = delta >> 7, delta & 127
-            first = pltpu.roll(joined[pl.ds(rows, 72), :], (LANES - lanes) & 127, 1)
-            second = pltpu.roll(joined[pl.ds(rows + 1, 72), :], (LANES - lanes) & 127, 1)
-            moved = jnp.where(lane < LANES - lanes, first, second)
+            here = pltpu.roll(joined[pl.ds(rows, 72), :], (LANES - lanes) & 127, 1)
+            after = pltpu.roll(joined[pl.ds(rows + 1, 72), :], (LANES - lanes) & 127, 1)
+            moved = jnp.where(lane < LANES - lanes, here, after)
             result = jnp.where(within, moved, result)
         out[a] = result
 
 
-def passed_along(array, axis, by):
-    count = lax.axis_size(axis)
-    pairs = [(i, i + by) for i in range(count) if 0 <= i + by < count]
-    return lax.ppermute(array, axis, pairs)
+def exchanged(array, axis, first):
+    pairs = [(i, i + 1) for i in range(first, lax.axis_size(axis) - 1, 2)]
+    return lax.ppermute(array, axis, pairs + [(b, a) for a, b in pairs])
 
 
 def shape(*dims, dtype=F32):
@@ -370,18 +378,24 @@
     vmem = pl.BlockSpec(memory_space=pltpu.VMEM)
     smem = pl.BlockSpec(memory_space=pltpu.SMEM)
     params = pltpu.CompilerParams(vmem_limit_bytes=VMEM)
-    masked, moments, *faces = pl.pallas_call(
+    masked, *sends = pl.pallas_call(
         prepare_kernel,
         in_specs=[vmem, vmem, vmem, smem],
-        out_shape=[shape(3, CELLS, LANES), shape(256, LANES)] + [shape(9, FACE, LANES)] * 6,
+        out_shape=[shape(3, CELLS, LANES)] + [shape(9, FACE, LANES)] * 6,
         compiler_params=params,
         name="prepare",
     )(offsets, burgers, lines, counts)
-    by_name = dict(zip(FACES, faces))
-    received = []
-    for axis, name in zip(AXES, "xyz"):
-        received.append(passed_along(by_name[name + "hi"], axis, 1))
-        received.append(passed_along(by_name[name + "lo"], axis, -1))
+    received = [None] * 6
+    for i in (1, 3, 5, 0, 2, 4):
+        received[i] = exchanged(sends[i], AXES[i // 2], i % 2)
+    masked, *received = lax.optimization_barrier((masked, *received))
+    moments = pl.pallas_call(
+        moments_kernel,
+        in_specs=[vmem, vmem],
+        out_shape=shape(256, LANES),
+        compiler_params=params,
+        name="moments",
+    )(masked, lines)
     gathered = lax.all_to_all(
         moments.reshape(256, 1, LANES), AXES, 0, 0, tiled=True
     ).reshape(256, LANES)
@@ -390,16 +404,16 @@
         in_specs=[vmem] * 9,
         out_shape=shape(CELLS, 3, LANES),
         scratch_shapes=[
-            pltpu.VMEM((SOURCES, LANES, LANES), F32),
-            pltpu.VMEM((CELLS, LANES, LANES), F32),
-            pltpu.VMEM((SOURCES, LANES, LANES), BF16),
-            pltpu.VMEM((CELLS, LANES, 2 * LANES), BF16),
+            pltpu.VMEM((SOURCES, DEPTH, LANES), F32),
+            pltpu.VMEM((CELLS, DEPTH, LANES), F32),
+            pltpu.VMEM((SOURCES, LANES, DEPTH), BF16),
+            pltpu.VMEM((CELLS, DEPTH, 2 * LANES), BF16),
             pltpu.VMEM((SOURCES, 16, LANES), BF16),
         ],
         compiler_params=params,
         name="near",
     )(offsets, masked, lines, *received)
-    fields, tail, head = pl.pallas_call(
+    fields, *ends = pl.pallas_call(
         node_kernel,
         in_specs=[vmem] * 4 + [smem] + [vmem] * 3,
         out_shape=[shape(6, 64, LANES), shape(6, 4, LANES), shape(6, 4, LANES)],
@@ -412,8 +426,8 @@
         compiler_params=params,
         name="nodes",
     )(gathered, near, masked, lines, stress, connect, node_pos, drag)
-    below = passed_along(tail, "gx", 1)
-    above = passed_along(head, "gx", -1)
+    second = exchanged(ends[1], "gx", 1)
+    first = exchanged(ends[0], "gx", 0)
     out = pl.pallas_call(
         migrate_kernel,
         in_specs=[vmem] * 3 + [smem],
@@ -421,7 +435,7 @@
         scratch_shapes=[pltpu.VMEM((96, LANES), F32)],
         compiler_params=params,
         name="migrate",
-    )(fields, below, above, shifts)
+    )(fields, first, second, shifts)
     return out.reshape(6, 1, 1, 1, 72 * LANES)
 
 

time: 119 us -> 84.8 us (0.71)
  Pallas kernels: 56.7 us -> 42.2 us
  starting transfers between devices: 46.2 us -> 36 us
  waiting for transfers between devices: 13.1 us -> 4.84 us
    pallas_call x1, Pallas kernels: 41.3 us -> 24.9 us  [shards(): pl.pallas_call(near_kernel, in_specs=[vmem] * 9, out_shape=shape(CELLS, 3...]
    ppermute x8, starting transfers between devices: 31.5 us -> 20.7 us  [exchanged(): return lax.ppermute(array, axis, pairs + [(b, a) for a, b in pairs])]
    ppermute x8, waiting for transfers between devices: 13.1 us -> 4.84 us  [exchanged(): return lax.ppermute(array, axis, pairs + [(b, a) for a, b in pairs])]
    pallas_call x0 -> x1, Pallas kernels: none -> 2.22 us  [shards(): pl.pallas_call(moments_kernel, in_specs=[vmem, vmem], out_shape=shape(256...]
  transfers between devices with their start and end apart: 9 -> 9, of which waited for: 3 -> 4; matrix products, arithmetic and copies ran while one was open for 0% -> 0% of each run, Pallas kernels for 35% -> 30%
where the time goes in v2:
time: 84.8 us; the launch traced here: 84.4 us
  Pallas kernels  42.2 us (50%)
  starting transfers between devices  36 us (42%)
  waiting for transfers between devices  4.84 us (6%)
  local copies, waits for them, and re-layouts  1.27 us (1%)
    pallas_call x1, Pallas kernels, shards(): pl.pallas_call(near_kernel, in_specs=[vmem] * 9, out_shape=shape(CELLS, 3...  24.9 us
    ppermute x8, starting transfers between devices, exchanged(): return lax.ppermute(array, axis, pairs + [(b, a) for a, b in pairs])  20.7 us
    all_to_all x1, starting transfers between devices, shards(): lax.all_to_all(moments.reshape(256, 1, LANES), AXES, 0, 0, tiled=True)  15.3 us
    pallas_call x1, Pallas kernels, shards(): pl.pallas_call(node_kernel, in_specs=[vmem] * 4 + [smem] + [vmem] * 3, ou...  11 us
    ppermute x8, waiting for transfers between devices, exchanged(): return lax.ppermute(array, axis, pairs + [(b, a) for a, b in pairs])  4.84 us
    pallas_call x1, Pallas kernels, shards(): pl.pallas_call(moments_kernel, in_specs=[vmem, vmem], out_shape=shape(256...  2.22 us
    pallas_call x1, Pallas kernels, shards(): pl.pallas_call(migrate_kernel, in_specs=[vmem] * 3 + [smem], out_shape=sh...  2.2 us
    pallas_call x1, Pallas kernels, shards(): pl.pallas_call(prepare_kernel, in_specs=[vmem, vmem, vmem, smem], out_sha...  1.82 us
  transfers between devices with their start and end apart: 9, of which 4 were waited for; matrix products, arithmetic and copies ran while one was open for 0% of the time, Pallas kernels for 30%

profile of v2, /device:TPU:25, one launch (start us, length us, event | category | flops | bytes accessed | tf_op | source)
XLA Modules:
  0.0 84.4 jit_solution(1263325091632533239)
XLA Ops:
  0.0 1.8 %prepare.1 = (f32[3,64,128]{2,1,0:T(8,128)}, f32[9,16,128]{2,1,0:T(8,128)}, f32[9,16,128]{2,1,0:T(8,128)}, f32[9,16,128]{2,1,0:T(8,128)}, f32[9,16,128]{2,1,0:T(...) custom-call(f32[3,64,128]{2,1,0:T(8,128)} %bitcast.18, f32[3,64,128]{2,1,0:T(8,128)} %bitcast.21, ...), custom_call_target="tpu_custom_call" | custom-call | tf_op jit(solution)/shard_map/prepare/pallas_call | solution.py:381
  1.8 0.7 collective-permute-start
  2.5 8.4 %collective-permute-start.1 = (f32[9,16,128]{2,1,0:T(8,128)}, f32[9,16,128]{2,1,0:T(8,128)S(1)}, u32[]{:S(2)}, u32[]{:S(2)}) collective-permute-start(f32[9,16,128]{2,1,0:T(8,128)} %get-tuple-element.24), channel_id=1, source_target_pairs={{16,32},{48,64},{80,96},{112,128},{144,160},{176,192},{208,224},{3... | collective-permute-start | bytes 221192 | tf_op jit(solution)/shard_map/ppermute | solution.py:363
  10.9 0.8 collective-permute-start.2
  11.7 0.7 collective-permute-start.3
  12.3 1.3 %collective-permute-start.4 = (f32[9,16,128]{2,1,0:T(8,128)}, f32[9,16,128]{2,1,0:T(8,128)S(1)}, u32[]{:S(2)}, u32[]{:S(2)}) collective-permute-start(f32[9,16,128]{2,1,0:T(8,128)} %get-tuple-element.27), channel_id=1, source_target_pairs={{0,1},{2,3},{1,0},{3,2},{4,5},{6,7},{5,4},{7,6},{8,9},{10,11},{9,8... | collective-permute-start | bytes 221192 | tf_op jit(solution)/shard_map/ppermute | solution.py:363
  13.6 0.0 collective-permute-done.refs_3_
  13.6 0.7 collective-permute-start.5
  14.3 0.4 collective-permute-done.1.refs_4_
  14.7 0.4 collective-permute-done.2.refs_5_
  15.2 0.0 collective-permute-done.3.refs_6_
  15.2 0.7 collective-permute-done.4.refs_7_
  15.8 0.0 collective-permute-done.5.refs_8_
  15.9 2.2 %moments.1 = f32[256,128]{1,0:T(8,128)} custom-call(f32[3,64,128]{2,1,0:T(8,128)} %get-tuple-element.29.masked.refs_1_, f32[3,64,128]{2,1,0:T(8,128)} %bitcast.13), custom_call_target="tpu_custom_call" | custom-call | tf_op jit(solution)/shard_map/moments/pallas_call | solution.py:392
  18.1 0.0 copy-done.1
  18.1 0.0 copy-done.2
  18.1 0.0 copy-done.3
  18.1 0.0 copy-done.4
  18.1 0.0 copy-done.5
  18.1 0.0 copy-done.6
  18.1 15.3 %all-to-all-start = ((f32[256,1,128]{2,1,0:T(1,128)}), f32[256,1,128]{2,1,0:T(1,128)S(1)}, u32[]{:S(2)}, u32[]{:S(2)}) async-start(f32[256,1,128]{2,1,0:T(1,128)} %bitcast.17), calls=%async_computation | async-start | bytes 262144 | tf_op jit(solution)/shard_map/all_to_all | solution.py:399
  33.4 24.9 %near.1 = f32[64,3,128]{2,1,0:T(4,128)} custom-call(f32[3,64,128]{2,1,0:T(8,128)} %bitcast.19, f32[3,64,128]{2,1,0:T(8,128)} %get-tuple-element.29.masked.refs_1_, f32[3,64,128]{2,1,0:T(8,128)} %bitcast.14, f32[9,16,128]{2,1,0:T(8,128)} %copy-done.1, f32[9,16,128]{2,1,0:T(8,128)} %copy-done.2, f32[9,16,128]{2,1,0:T(8,128)} %copy-done.3, ...), custom_call_target="tpu_custom_call" | custom-call | tf_op jit(solution)/shard_map/near/pallas_call | solution.py:402
  58.3 0.0 all-to-all-done
  58.3 0.7 copy-done
  59.0 11.0 %nodes.1 = (f32[6,64,128]{2,1,0:T(8,128)}, f32[6,4,128]{2,1,0:T(4,128)}, f32[6,4,128]{2,1,0:T(4,128)}) custom-call(f32[256,128]{1,0:T(8,128)} %bitcast.16, f32[64,3,128]{2,1,0:T(4,128)} %near.1, f32[3,64,128]{2,1,0:T(8,128)} %get-tuple-element.29.masked.refs_1_, f32[3,64,128]{2,1,0:T(8,128)} %bitcast.15, f32[3,3]{1,0:T(4,128)} %stress.1, ...), custom_call_target="tpu_custom_call" | custom-call | tf_op jit(solution)/shard_map/nodes/pallas_call | solution.py:416
  70.0 0.4 collective-permute-start.6
  70.4 7.9 %collective-permute-start.7 = (f32[6,4,128]{2,1,0:T(4,128)}, f32[6,4,128]{2,1,0:T(4,128)S(1)}, u32[]{:S(2)}, u32[]{:S(2)}) collective-permute-start(f32[6,4,128]{2,1,0:T(4,128)} %get-tuple-element.38), channel_id=1, source_target_pairs={{16,32},{48,64},{80,96},{112,128},{144,160},{176,192},{208,224},{3... | collective-permute-start | bytes 36872 | tf_op jit(solution)/shard_map/ppermute | solution.py:363
  78.3 0.0 collective-permute-done.6.first
  78.3 0.0 copy-start.7
  78.3 3.3 %collective-permute-done.7.second = f32[6,4,128]{2,1,0:T(4,128)S(1)} collective-permute-done((f32[6,4,128]{2,1,0:T(4,128)}, f32[6,4,128]{2,1,0:T(4,128)S(1)}, u32[]{:S(2)}, u32[]{:S(2)}) %collective-permute-start.7) | collective-permute-done | bytes 12320 | tf_op jit(solution)/shard_map/ppermute | solution.py:363
  81.6 0.6 copy-done.8
  82.2 2.2 %migrate.1 = f32[6,72,128]{2,1,0:T(8,128)} custom-call(f32[6,64,128]{2,1,0:T(8,128)} %get-tuple-element.36.fields, f32[6,4,128]{2,1,0:T(4,128)} %copy-done.7, f32[6,4,128]{2,1,0:T(4,128)} %copy-done.8, s32[2,4,4,16]{3,2,1,0:T(4,128)} %bitcast.24), custom_call_target="tpu_custom_call" | custom-call | tf_op jit(solution)/shard_map/migrate/pallas_call | solution.py:431
  (9 shorter events, 0.0 us)
Async XLA Ops:
  1.8 11.8 %collective-permute-start = (f32[9,16,128]{2,1,0:T(8,128)}, f32[9,16,128]{2,1,0:T(8,128)S(1)}, u32[]{:S(2)}, u32[]{:S(2)}) collective-permute-start(f32[9,16,128]{2,1,0:T(8,128)} %get-tuple-element.23), channel_id=1, source_target_pairs={{0,16},{32,48},{64,80},{96,112},{128,144},{160,176},{192,208},{224... | collective-permute-start | bytes 221192 | tf_op jit(solution)/shard_map/ppermute | solution.py:363
  2.5 12.2 %collective-permute-start.1 = (f32[9,16,128]{2,1,0:T(8,128)}, f32[9,16,128]{2,1,0:T(8,128)S(1)}, u32[]{:S(2)}, u32[]{:S(2)}) collective-permute-start(f32[9,16,128]{2,1,0:T(8,128)} %get-tuple-element.24), channel_id=1, source_target_pairs={{16,32},{48,64},{80,96},{112,128},{144,160},{176,192},{208,224},{3... | collective-permute-start | bytes 221192 | tf_op jit(solution)/shard_map/ppermute | solution.py:363
  10.9 4.3 %collective-permute-start.2 = (f32[9,16,128]{2,1,0:T(8,128)}, f32[9,16,128]{2,1,0:T(8,128)S(1)}, u32[]{:S(2)}, u32[]{:S(2)}) collective-permute-start(f32[9,16,128]{2,1,0:T(8,128)} %get-tuple-element.25), channel_id=1, source_target_pairs={{0,4},{8,12},{4,0},{12,8},{1,5},{9,13},{5,1},{13,9},{2,6},{10,14},... | collective-permute-start | bytes 221192 | tf_op jit(solution)/shard_map/ppermute | solution.py:363
  11.7 3.5 %collective-permute-start.3 = (f32[9,16,128]{2,1,0:T(8,128)}, f32[9,16,128]{2,1,0:T(8,128)S(1)}, u32[]{:S(2)}, u32[]{:S(2)}) collective-permute-start(f32[9,16,128]{2,1,0:T(8,128)} %get-tuple-element.26), channel_id=1, source_target_pairs={{4,8},{8,4},{5,9},{9,5},{6,10},{10,6},{7,11},{11,7},{20,24},{24,20... | collective-permute-start | bytes 221192 | tf_op jit(solution)/shard_map/ppermute | solution.py:363
  12.3 3.5 %collective-permute-start.4 = (f32[9,16,128]{2,1,0:T(8,128)}, f32[9,16,128]{2,1,0:T(8,128)S(1)}, u32[]{:S(2)}, u32[]{:S(2)}) collective-permute-start(f32[9,16,128]{2,1,0:T(8,128)} %get-tuple-element.27), channel_id=1, source_target_pairs={{0,1},{2,3},{1,0},{3,2},{4,5},{6,7},{5,4},{7,6},{8,9},{10,11},{9,8... | collective-permute-start | bytes 221192 | tf_op jit(solution)/shard_map/ppermute | solution.py:363
  13.6 4.4 %copy-start.1 = (f32[9,16,128]{2,1,0:T(8,128)}, f32[9,16,128]{2,1,0:T(8,128)S(1)}, u32[]{:S(2)}) copy-start(f32[9,16,128]{2,1,0:T(8,128)S(1)} %collective-permute-done.refs_3_) | copy-start | bytes 221188
  13.6 2.2 %collective-permute-start.5 = (f32[9,16,128]{2,1,0:T(8,128)}, f32[9,16,128]{2,1,0:T(8,128)S(1)}, u32[]{:S(2)}, u32[]{:S(2)}) collective-permute-start(f32[9,16,128]{2,1,0:T(8,128)} %get-tuple-element.28), channel_id=1, source_target_pairs={{1,2},{2,1},{5,6},{6,5},{9,10},{10,9},{13,14},{14,13},{17,18},{18,... | collective-permute-start | bytes 221192 | tf_op jit(solution)/shard_map/ppermute | solution.py:363
  14.7 3.4 %copy-start.2 = (f32[9,16,128]{2,1,0:T(8,128)}, f32[9,16,128]{2,1,0:T(8,128)S(1)}, u32[]{:S(2)}) copy-start(f32[9,16,128]{2,1,0:T(8,128)S(1)} %collective-permute-done.1.refs_4_) | copy-start | bytes 221188
  15.2 2.9 %copy-start.3 = (f32[9,16,128]{2,1,0:T(8,128)}, f32[9,16,128]{2,1,0:T(8,128)S(1)}, u32[]{:S(2)}) copy-start(f32[9,16,128]{2,1,0:T(8,128)S(1)} %collective-permute-done.2.refs_5_) | copy-start | bytes 221188
  15.2 2.9 %copy-start.4 = (f32[9,16,128]{2,1,0:T(8,128)}, f32[9,16,128]{2,1,0:T(8,128)S(1)}, u32[]{:S(2)}) copy-start(f32[9,16,128]{2,1,0:T(8,128)S(1)} %collective-permute-done.3.refs_6_) | copy-start | bytes 221188
  15.8 2.2 %copy-start.5 = (f32[9,16,128]{2,1,0:T(8,128)}, f32[9,16,128]{2,1,0:T(8,128)S(1)}, u32[]{:S(2)}) copy-start(f32[9,16,128]{2,1,0:T(8,128)S(1)} %collective-permute-done.4.refs_7_) | copy-start | bytes 221188
  15.9 2.3 %copy-start.6 = (f32[9,16,128]{2,1,0:T(8,128)}, f32[9,16,128]{2,1,0:T(8,128)S(1)}, u32[]{:S(2)}) copy-start(f32[9,16,128]{2,1,0:T(8,128)S(1)} %collective-permute-done.5.refs_8_) | copy-start | bytes 221188
  18.1 40.2 %all-to-all-start = ((f32[256,1,128]{2,1,0:T(1,128)}), f32[256,1,128]{2,1,0:T(1,128)S(1)}, u32[]{:S(2)}, u32[]{:S(2)}) async-start(f32[256,1,128]{2,1,0:T(1,128)} %bitcast.17), calls=%async_computation | async-start | bytes 262144 | tf_op jit(solution)/shard_map/all_to_all | solution.py:399
  58.3 0.7 copy-start
  70.0 8.3 %collective-permute-start.6 = (f32[6,4,128]{2,1,0:T(4,128)}, f32[6,4,128]{2,1,0:T(4,128)S(1)}, u32[]{:S(2)}, u32[]{:S(2)}) collective-permute-start(f32[6,4,128]{2,1,0:T(4,128)} %get-tuple-element.37), channel_id=1, source_target_pairs={{0,16},{32,48},{64,80},{96,112},{128,144},{160,176},{192,208},{224... | collective-permute-start | bytes 36872 | tf_op jit(solution)/shard_map/ppermute | solution.py:363
  70.4 11.2 %collective-permute-start.7 = (f32[6,4,128]{2,1,0:T(4,128)}, f32[6,4,128]{2,1,0:T(4,128)S(1)}, u32[]{:S(2)}, u32[]{:S(2)}) collective-permute-start(f32[6,4,128]{2,1,0:T(4,128)} %get-tuple-element.38), channel_id=1, source_target_pairs={{16,32},{48,64},{80,96},{112,128},{144,160},{176,192},{208,224},{3... | collective-permute-start | bytes 36872 | tf_op jit(solution)/shard_map/ppermute | solution.py:363
  78.3 3.3 %copy-start.7 = (f32[6,4,128]{2,1,0:T(4,128)}, f32[6,4,128]{2,1,0:T(4,128)S(1)}, u32[]{:S(2)}) copy-start(f32[6,4,128]{2,1,0:T(4,128)S(1)} %collective-permute-done.6.first) | copy-start | bytes 36868
  81.6 0.6 copy-start.8

commit v3 on v2

--- a/solution.py
+++ b/solution.py
@@ -30,6 +30,11 @@
     )[axis]
 
 
+def split2(value):
+    high = value.astype(BF16).astype(F32)
+    return high, value - high
+
+
 def split3(value):
     high = value.astype(BF16).astype(F32)
     rest = value - high
@@ -37,7 +42,7 @@
     return high, middle, rest - middle
 
 
-def prepare_kernel(offsets, burgers, lines, counts, masked, *sends):
+def prepare_kernel(offsets, burgers, lines, counts, masked, moments, *sends):
     slot = lax.broadcasted_iota(jnp.int32, (8, LANES), 1)
     row = lax.broadcasted_iota(jnp.int32, (8, LANES), 0)
     for group in range(8):
@@ -64,9 +69,6 @@
                         even, of_low, of_high
                     )
             to += size
-
-
-def moments_kernel(masked, lines, moments):
     rows = []
     for coarse in range(4):
         big_x, big_y = coarse // 2, coarse % 2
@@ -96,11 +98,8 @@
     moments[...] = jnp.broadcast_to(packed[0:1], moments.shape)
 
 
-def source_index(target):
+def source_index(target, lower, upper):
     x, y, z = target >> 4, (target >> 2) & 3, target & 3
-    odd = [lax.axis_index(a) & 1 for a in AXES]
-    upper = [CELLS + 2 * FACE * a + FACE * odd[a] for a in range(3)]
-    lower = [CELLS + 2 * FACE * a + FACE * (1 - odd[a]) for a in range(3)]
     return [
         target,
         jnp.where(x > 0, target - 16, lower[0] + (target & 15)),
@@ -119,7 +118,7 @@
     offsets, masked, lines = refs[:3]
     faces = refs[3:9]
     near = refs[9]
-    rows_s, rows_t, source, target, points = refs[10:]
+    rows_s, rows_t, source, points = refs[10:]
     blocks = []
     for first in range(0, CELLS, 16):
         cell = first + lax.broadcasted_iota(jnp.int32, (16, LANES), 0)
@@ -185,43 +184,68 @@
                     rows_t[pl.ds(first, 16), k, :] = outer[ab][t]
                 k += 1
 
-    def arrange(c, carry):
+    odd = [lax.axis_index(a) & 1 for a in AXES]
+    upper = [CELLS + 2 * FACE * a + FACE * odd[a] for a in range(3)]
+    lower = [CELLS + 2 * FACE * a + FACE * (1 - odd[a]) for a in range(3)]
+
+    def arrange(c):
         block = rows_s[c]
         source[c] = block.astype(BF16).T
-        head = block[0:24]
         points[c] = jnp.concatenate(
-            [head[0:3], head[6:9], head[12:15], head[21:22], jnp.zeros((6, LANES), F32)], axis=0
+            [block[0:3], block[6:9], block[12:15], block[21:22], jnp.zeros((6, LANES), F32)],
+            axis=0,
         ).astype(BF16)
+
+    together = 8
+
+    def faces_of(i):
+        h, x = i & 1, i >> 1
+        y_face = jnp.where(h == 0, lower[1], upper[1]) + 4 * x
+        z_lower, z_upper = lower[2] + 2 * i, upper[2] + 2 * i
+        return [y_face + k for k in range(4)] + [z_lower, z_lower + 1, z_upper, z_upper + 1]
+
+    def first_own(k, carry):
+        arrange(k)
         return carry
 
-    lax.fori_loop(0, SOURCES, arrange, 0, unroll=8)
-
-    def arrange_target(c, carry):
-        block = rows_t[c]
-        row = lax.broadcasted_iota(jnp.int32, (DEPTH, LANES), 0)
-        target[c, :, :LANES] = jnp.where(row < 24, block, 0.0).astype(BF16)
-        target[c, :, LANES:] = jnp.where(row < 24, 0.0, block).astype(BF16)
+    def first_lower(k, carry):
+        arrange(lower[0] + k)
         return carry
 
-    lax.fori_loop(0, CELLS, arrange_target, 0, unroll=4)
-    together = 2
+    lax.fori_loop(0, 24, first_own, 0, unroll=8)
+    lax.fori_loop(0, FACE, first_lower, 0, unroll=8)
+    for c in faces_of(0):
+        arrange(c)
+    row = lax.broadcasted_iota(jnp.int32, (DEPTH, LANES), 0)
 
     def step(i, carry):
-        cells = [i * together + u for u in range(together)]
-        sources = [source_index(c) for c in cells]
-        stationary = [target[c] for c in cells]
-        weights = [[] for _ in cells]
-        spots = [[] for _ in cells]
-        for k in range(7):
-            for u in range(together):
-                pair = jnp.dot(source[sources[u][k]], stationary[u], preferred_element_type=F32)
+        following = jnp.minimum(i + 1, CELLS // together - 1)
+        ahead = jnp.where(
+            following < 6, 8 * following + 16, upper[0] + 8 * (following & 1)
+        )
+        coming = [ahead + k for k in range(8)] + faces_of(following)
+        weights = []
+        spots = []
+        for u in range(together):
+            cell = i * together + u
+            sources = source_index(cell, lower, upper)
+            block = rows_t[cell]
+            stationary = jnp.concatenate(
+                [jnp.where(row < 24, block, 0.0), jnp.where(row < 24, 0.0, block)], axis=1
+            ).astype(BF16)
+            weights.append([])
+            for k in range(7):
+                pair = jnp.dot(source[sources[k]], stationary, preferred_element_type=F32)
                 inverse = lax.rsqrt(pair[:, :LANES])
                 weight = pair[:, LANES:] * (inverse * inverse * inverse)
                 high = weight.astype(BF16)
                 low = (weight - high.astype(F32)).astype(BF16)
                 weights[u].append(jnp.concatenate([high, low], axis=1))
-                spots[u].append(points[sources[u][k]])
+            spots.append([points[c] for c in sources])
+            for c in coming[2 * u : 2 * u + 2]:
+                arrange(c)
         for u in range(together):
+            cell = i * together + u
             both = jnp.dot(
                 jnp.concatenate(spots[u], axis=1),
                 jnp.concatenate(weights[u], axis=0),
@@ -229,10 +253,9 @@
             )
             sums = both[:, :LANES] + both[:, LANES:]
             moved = sums[0:3] + sums[3:6] + sums[6:9]
-            total = sums[9:10]
-            base = rows_t[cells[u], 0:24, :]
+            base = rows_t[cell, 0:24, :]
             place = -0.5 * (base[0:3] + base[3:6] + base[9:12])
-            near[cells[u]] = place * total - moved
+            near[cell] = place * sums[9:10] - moved
         return carry
 
     lax.fori_loop(0, CELLS // together, step, 0)
@@ -240,7 +263,7 @@
 
 def node_kernel(
     gathered, near, masked, lines, stress, connect, node_pos, drag, fields, first, second,
-    values, sums, left, right,
+    values, sums,
 ):
     index_x, index_y, index_z = (lax.axis_index(a) for a in AXES)
     device = lax.broadcasted_iota(jnp.int32, (CELLS, 256), 1)
@@ -275,40 +298,39 @@
     for a in range(3):
         b, c = (a + 1) % 3, (a + 2) % 3
         force = NEAR_SCALE * near[:, a, :] + (pulled[b] * line[c] - pulled[c] * line[b])
-        parts = split3(0.5 * force)
-        for p in range(3):
-            values[3 * p + a] = parts[p]
+        high, rest = split2(0.5 * force)
+        values[a] = high
+        values[3 + a] = rest
     sums[...] = jnp.zeros(sums.shape, F32)
     rows_high = lax.broadcasted_iota(jnp.int32, (32, LANES), 0)
     rows_low = lax.broadcasted_iota(jnp.int32, (256, LANES), 0)
-    step_cells = 4
+    step_cells = 16
 
     def scatter(i, carry):
+        left, right = [], []
         for u in range(step_cells):
             at = i * step_cells + u
             for end in range(2):
-                column = (2 * u + end) * LANES
                 node = connect[end, pl.ds(at, 1), :]
                 chosen = rows_high == (node >> 8)
-                for q in range(9):
-                    left[pl.ds(32 * q, 32), pl.ds(column, LANES)] = jnp.where(
-                        chosen, values[q, pl.ds(at, 1), :], 0.0
+                left.append(
+                    jnp.concatenate(
+                        [jnp.where(chosen, values[q, pl.ds(at, 1), :], 0.0) for q in range(6)],
+                        axis=0,
                     ).astype(BF16)
-                right[:, pl.ds(column, LANES)] = (
-                    (rows_low == (node & 255)).astype(F32).astype(BF16)
                 )
+                right.append((rows_low == (node & 255)).astype(F32).astype(BF16))
         sums[...] += lax.dot_general(
-            left[...], right[...], (((1,), (1,)), ((), ())), preferred_element_type=F32
+            jnp.concatenate(left, axis=1),
+            jnp.concatenate(right, axis=1),
+            (((1,), (1,)), ((), ())),
+            preferred_element_type=F32,
         )
         return carry
 
-    lax.fori_loop(0, CELLS // step_cells, scatter, 0)
+    lax.fori_loop(0, CELLS // step_cells, scatter, 0, unroll=1)
     for a in range(3):
-        force = (
-            sums[pl.ds(32 * a, 32), :]
-            + sums[pl.ds(96 + 32 * a, 32), :]
-            + sums[pl.ds(192 + 32 * a, 32), :]
-        )
+        force = sums[pl.ds(32 * a, 32), :] + sums[pl.ds(96 + 32 * a, 32), :]
         fields[3 + a, pl.ds(0, 32, stride=2), :] = force[:, :LANES]
         fields[3 + a, pl.ds(1, 32, stride=2), :] = force[:, LANES:]
     for a in range(3):
@@ -364,7 +386,11 @@
 
 
 def shape(*dims, dtype=F32):
-    return jax.ShapeDtypeStruct(dims, dtype)
+    return pltpu.VMEM(dims, dtype)
+
+
+def on_chip(array):
+    return pltpu.with_memory_space_constraint(array, pltpu.VMEM)
 
 
 def shards(offsets, burgers, lines, counts, connect, node_pos, drag, stress, shifts):
@@ -378,24 +404,17 @@
     vmem = pl.BlockSpec(memory_space=pltpu.VMEM)
     smem = pl.BlockSpec(memory_space=pltpu.SMEM)
     params = pltpu.CompilerParams(vmem_limit_bytes=VMEM)
-    masked, *sends = pl.pallas_call(
+    masked, moments, *sends = pl.pallas_call(
         prepare_kernel,
         in_specs=[vmem, vmem, vmem, smem],
-        out_shape=[shape(3, CELLS, LANES)] + [shape(9, FACE, LANES)] * 6,
+        out_shape=[shape(3, CELLS, LANES), shape(256, LANES)] + [shape(9, FACE, LANES)] * 6,
         compiler_params=params,
         name="prepare",
     )(offsets, burgers, lines, counts)
     received = [None] * 6
     for i in (1, 3, 5, 0, 2, 4):
         received[i] = exchanged(sends[i], AXES[i // 2], i % 2)
-    masked, *received = lax.optimization_barrier((masked, *received))
-    moments = pl.pallas_call(
-        moments_kernel,
-        in_specs=[vmem, vmem],
-        out_shape=shape(256, LANES),
-        compiler_params=params,
-        name="moments",
-    )(masked, lines)
+    moments, *received = lax.optimization_barrier((moments, *received))
     gathered = lax.all_to_all(
         moments.reshape(256, 1, LANES), AXES, 0, 0, tiled=True
     ).reshape(256, LANES)
@@ -407,35 +426,32 @@
             pltpu.VMEM((SOURCES, DEPTH, LANES), F32),
             pltpu.VMEM((CELLS, DEPTH, LANES), F32),
             pltpu.VMEM((SOURCES, LANES, DEPTH), BF16),
-            pltpu.VMEM((CELLS, DEPTH, 2 * LANES), BF16),
             pltpu.VMEM((SOURCES, 16, LANES), BF16),
         ],
         compiler_params=params,
         name="near",
-    )(offsets, masked, lines, *received)
+    )(offsets, on_chip(masked), lines, *[on_chip(face) for face in received])
     fields, *ends = pl.pallas_call(
         node_kernel,
         in_specs=[vmem] * 4 + [smem] + [vmem] * 3,
         out_shape=[shape(6, 64, LANES), shape(6, 4, LANES), shape(6, 4, LANES)],
         scratch_shapes=[
-            pltpu.VMEM((9, CELLS, LANES), F32),
-            pltpu.VMEM((288, 256), F32),
-            pltpu.VMEM((288, 1024), BF16),
-            pltpu.VMEM((256, 1024), BF16),
+            pltpu.VMEM((6, CELLS, LANES), F32),
+            pltpu.VMEM((192, 256), F32),
         ],
         compiler_params=params,
         name="nodes",
-    )(gathered, near, masked, lines, stress, connect, node_pos, drag)
+    )(on_chip(gathered), on_chip(near), on_chip(masked), lines, stress, connect, node_pos, drag)
     second = exchanged(ends[1], "gx", 1)
     first = exchanged(ends[0], "gx", 0)
     out = pl.pallas_call(
         migrate_kernel,
         in_specs=[vmem] * 3 + [smem],
-        out_shape=shape(6, 72, LANES),
+        out_shape=jax.ShapeDtypeStruct((6, 72, LANES), F32),
         scratch_shapes=[pltpu.VMEM((96, LANES), F32)],
         compiler_params=params,
         name="migrate",
-    )(fields, first, second, shifts)
+    )(on_chip(fields), on_chip(first), on_chip(second), shifts)
     return out.reshape(6, 1, 1, 1, 72 * LANES)
 
 

time: 84.8 us -> 69.8 us (0.82)
  Pallas kernels: 42.2 us -> 28.8 us
  local copies, waits for them, and re-layouts: 1.27 us -> 0 us
    pallas_call x1, Pallas kernels: 24.9 us -> 19 us  [shards(): pl.pallas_call(near_kernel, in_specs=[vmem] * 9, out_shape=shape(CELLS, 3...]
    pallas_call x1, Pallas kernels: 11 us -> 5.45 us  [shards(): pl.pallas_call(node_kernel, in_specs=[vmem] * 4 + [smem] + [vmem] * 3, ou...]
    pallas_call x2 -> x1, Pallas kernels: 4.41 us -> 2.06 us  [shards(): pl.pallas_call(migrate_kernel, in_specs=[vmem] * 3 + [smem], out_shape=ja...]
    unnamed x18 -> x0, local copies, waits for them, and re-layouts: 1.27 us -> none
  transfers between devices with their start and end apart: 9 -> 9, of which waited for: 4 -> 4; matrix products, arithmetic and copies ran while one was open for 0% -> 0% of each run, Pallas kernels for 30% -> 27%
where the time goes in v3:
time: 69.8 us; the launch traced here: 69.4 us
  starting transfers between devices  36.1 us (52%)
  Pallas kernels  28.8 us (41%)
  waiting for transfers between devices  4.42 us (6%)
    ppermute x8, starting transfers between devices, exchanged(): return lax.ppermute(array, axis, pairs + [(b, a) for a, b in pairs])  20.8 us
    pallas_call x1, Pallas kernels, shards(): pl.pallas_call(near_kernel, in_specs=[vmem] * 9, out_shape=shape(CELLS, 3...  19 us
    all_to_all x1, starting transfers between devices, shards(): lax.all_to_all(moments.reshape(256, 1, LANES), AXES, 0, 0, tiled=True)  15.3 us
    pallas_call x1, Pallas kernels, shards(): pl.pallas_call(node_kernel, in_specs=[vmem] * 4 + [smem] + [vmem] * 3, ou...  5.45 us
    ppermute x8, waiting for transfers between devices, exchanged(): return lax.ppermute(array, axis, pairs + [(b, a) for a, b in pairs])  4.42 us
    pallas_call x1, Pallas kernels, shards(): pl.pallas_call(prepare_kernel, in_specs=[vmem, vmem, vmem, smem], out_sha...  2.27 us
    pallas_call x1, Pallas kernels, shards(): pl.pallas_call(migrate_kernel, in_specs=[vmem] * 3 + [smem], out_shape=ja...  2.06 us
  transfers between devices with their start and end apart: 9, of which 4 were waited for; matrix products, arithmetic and copies ran while one was open for 0% of the time, Pallas kernels for 27%

profile of v3, /device:TPU:25, one launch (start us, length us, event | category | flops | bytes accessed | tf_op | source)
XLA Modules:
  0.0 69.4 jit_solution(16359312221496932245)
XLA Ops:
  0.0 2.3 %prepare.1 = (f32[3,64,128]{2,1,0:T(8,128)S(1)}, f32[256,128]{1,0:T(8,128)}, f32[9,16,128]{2,1,0:T(8,128)S(1)}, f32[9,16,128]{2,1,0:T(8,128)S(1)}, f32[9,16,128]...) custom-call(f32[3,64,128]{2,1,0:T(8,128)} %bitcast.16, ...), custom_call_target="tpu_custom_call" | custom-call | tf_op jit(solution)/shard_map/prepare/pallas_call | solution.py:407
  2.3 0.7 collective-permute-start
  2.9 8.4 %collective-permute-start.1 = (f32[9,16,128]{2,1,0:T(8,128)S(1)}, f32[9,16,128]{2,1,0:T(8,128)S(1)}, u32[]{:S(2)}, u32[]{:S(2)}) collective-permute-start(f32[9,16,128]{2,1,0:T(8,128)S(1)} %get-tuple-element.25), channel_id=1, source_target_pairs={{16,32},{48,64},{80,96},{112,128},{144,160},{176,192},{208,224},{3... | collective-permute-start | bytes 221192 | tf_op jit(solution)/shard_map/ppermute | solution.py:385
  11.3 0.8 %collective-permute-start.2 = (f32[9,16,128]{2,1,0:T(8,128)S(1)}, f32[9,16,128]{2,1,0:T(8,128)S(1)}, u32[]{:S(2)}, u32[]{:S(2)}) collective-permute-start(f32[9,16,128]{2,1,0:T(8,128)S(1)} %get-tuple-element.26), channel_id=1, source_target_pairs={{0,4},{8,12},{4,0},{12,8},{1,5},{9,13},{5,1},{13,9},{2,6},{10,14},... | collective-permute-start | bytes 221192 | tf_op jit(solution)/shard_map/ppermute | solution.py:385
  12.1 0.7 collective-permute-start.3
  12.8 1.3 %collective-permute-start.4 = (f32[9,16,128]{2,1,0:T(8,128)S(1)}, f32[9,16,128]{2,1,0:T(8,128)S(1)}, u32[]{:S(2)}, u32[]{:S(2)}) collective-permute-start(f32[9,16,128]{2,1,0:T(8,128)S(1)} %get-tuple-element.28), channel_id=1, source_target_pairs={{0,1},{2,3},{1,0},{3,2},{4,5},{6,7},{5,4},{7,6},{8,9},{10,11},{9,8... | collective-permute-start | bytes 221192 | tf_op jit(solution)/shard_map/ppermute | solution.py:385
  14.1 0.0 collective-permute-done.refs_3_
  14.1 0.7 collective-permute-start.5
  14.8 0.2 collective-permute-done.1.refs_4_
  14.9 0.5 collective-permute-done.2.refs_5_
  15.4 0.0 collective-permute-done.3.refs_6_
  15.4 0.7 collective-permute-done.4.refs_7_
  16.1 0.0 collective-permute-done.5.refs_8_
  16.1 15.3 %all-to-all-start = ((f32[256,1,128]{2,1,0:T(1,128)}), f32[256,1,128]{2,1,0:T(1,128)S(1)}, u32[]{:S(2)}, u32[]{:S(2)}) async-start(f32[256,1,128]{2,1,0:T(1,128)} %bitcast.4), calls=%async_computation | async-start | bytes 262144 | tf_op jit(solution)/shard_map/all_to_all | solution.py:418
  31.4 19.0 %near.1 = f32[64,3,128]{2,1,0:T(4,128)S(1)} custom-call(f32[3,64,128]{2,1,0:T(8,128)} %bitcast.17, f32[3,64,128]{2,1,0:T(8,128)S(1)} %get-tuple-element.31.refs_1_.masked, f32[3,64,128]{2,1,0:T(8,128)} %bitcast.14, f32[9,16,128]{2,1,0:T(8,128)S(1)} %collective-permute-done.refs_3_, f32[9,16,128]{2,1,0:T(8,128)S(1)} %collective-permute-done.1.refs_4_, ...), custom_call_target="tpu_custom_call" | custom-call | tf_op jit(solution)/shard_map/near/pallas_call | solution.py:421
  50.4 0.0 all-to-all-done
  50.4 5.4 %nodes.1 = (f32[6,64,128]{2,1,0:T(8,128)S(1)}, f32[6,4,128]{2,1,0:T(4,128)S(1)}, f32[6,4,128]{2,1,0:T(4,128)S(1)}) custom-call(f32[256,128]{1,0:T(8,128)S(1)} %bitcast.12, f32[64,3,128]{2,1,0:T(4,128)S(1)} %near.1, f32[3,64,128]{2,1,0:T(8,128)S(1)} %get-tuple-element.31.refs_1_.masked, f32[3,64,128]{2,1,0:T(8,128)} %bitcast.15, f32[3,3]{1,0:T(4,128)} %stress.1, ...), custom_call_target="tpu_custom_call" | custom-call | tf_op jit(solution)/shard_map/nodes/pallas_call | solution.py:434
  55.9 0.4 collective-permute-start.6
  56.3 7.9 %collective-permute-start.7 = (f32[6,4,128]{2,1,0:T(4,128)S(1)}, f32[6,4,128]{2,1,0:T(4,128)S(1)}, u32[]{:S(2)}, u32[]{:S(2)}) collective-permute-start(f32[6,4,128]{2,1,0:T(4,128)S(1)} %get-tuple-element.40), channel_id=1, source_target_pairs={{16,32},{48,64},{80,96},{112,128},{144,160},{176,192},{208,224},{3... | collective-permute-start | bytes 36872 | tf_op jit(solution)/shard_map/ppermute | solution.py:385
  64.3 0.0 collective-permute-done.6.first
  64.3 3.1 %collective-permute-done.7.second = f32[6,4,128]{2,1,0:T(4,128)S(1)} collective-permute-done((f32[6,4,128]{2,1,0:T(4,128)S(1)}, f32[6,4,128]{2,1,0:T(4,128)S(1)}, u32[]{:S(2)}, u32[]{:S(2)}) %collective-permute-start.7) | collective-permute-done | bytes 12320 | tf_op jit(solution)/shard_map/ppermute | solution.py:385
  67.3 2.1 %migrate.1 = f32[6,72,128]{2,1,0:T(8,128)} custom-call(f32[6,64,128]{2,1,0:T(8,128)S(1)} %get-tuple-element.38.fields, f32[6,4,128]{2,1,0:T(4,128)S(1)} %collective-permute-done.6.first, f32[6,4,128]{2,1,0:T(4,128)S(1)} %collective-permute-done.7.second, s32[2,4,4,16]{3,2,1,0:T(4,128)} %bitcast.22), custom_call_target="tpu_custom_call" | custom-call | tf_op jit(solution)/shard_map/migrate/pallas_call | solution.py:447
Async XLA Ops:
  2.3 11.8 %collective-permute-start = (f32[9,16,128]{2,1,0:T(8,128)S(1)}, f32[9,16,128]{2,1,0:T(8,128)S(1)}, u32[]{:S(2)}, u32[]{:S(2)}) collective-permute-start(f32[9,16,128]{2,1,0:T(8,128)S(1)} %get-tuple-element.24), channel_id=1, source_target_pairs={{0,16},{32,48},{64,80},{96,112},{128,144},{160,176},{192,208},{224... | collective-permute-start | bytes 221192 | tf_op jit(solution)/shard_map/ppermute | solution.py:385
  2.9 12.0 %collective-permute-start.1 = (f32[9,16,128]{2,1,0:T(8,128)S(1)}, f32[9,16,128]{2,1,0:T(8,128)S(1)}, u32[]{:S(2)}, u32[]{:S(2)}) collective-permute-start(f32[9,16,128]{2,1,0:T(8,128)S(1)} %get-tuple-element.25), channel_id=1, source_target_pairs={{16,32},{48,64},{80,96},{112,128},{144,160},{176,192},{208,224},{3... | collective-permute-start | bytes 221192 | tf_op jit(solution)/shard_map/ppermute | solution.py:385
  11.3 4.1 %collective-permute-start.2 = (f32[9,16,128]{2,1,0:T(8,128)S(1)}, f32[9,16,128]{2,1,0:T(8,128)S(1)}, u32[]{:S(2)}, u32[]{:S(2)}) collective-permute-start(f32[9,16,128]{2,1,0:T(8,128)S(1)} %get-tuple-element.26), channel_id=1, source_target_pairs={{0,4},{8,12},{4,0},{12,8},{1,5},{9,13},{5,1},{13,9},{2,6},{10,14},... | collective-permute-start | bytes 221192 | tf_op jit(solution)/shard_map/ppermute | solution.py:385
  12.1 3.3 %collective-permute-start.3 = (f32[9,16,128]{2,1,0:T(8,128)S(1)}, f32[9,16,128]{2,1,0:T(8,128)S(1)}, u32[]{:S(2)}, u32[]{:S(2)}) collective-permute-start(f32[9,16,128]{2,1,0:T(8,128)S(1)} %get-tuple-element.27), channel_id=1, source_target_pairs={{4,8},{8,4},{5,9},{9,5},{6,10},{10,6},{7,11},{11,7},{20,24},{24,20... | collective-permute-start | bytes 221192 | tf_op jit(solution)/shard_map/ppermute | solution.py:385
  12.8 3.3 %collective-permute-start.4 = (f32[9,16,128]{2,1,0:T(8,128)S(1)}, f32[9,16,128]{2,1,0:T(8,128)S(1)}, u32[]{:S(2)}, u32[]{:S(2)}) collective-permute-start(f32[9,16,128]{2,1,0:T(8,128)S(1)} %get-tuple-element.28), channel_id=1, source_target_pairs={{0,1},{2,3},{1,0},{3,2},{4,5},{6,7},{5,4},{7,6},{8,9},{10,11},{9,8... | collective-permute-start | bytes 221192 | tf_op jit(solution)/shard_map/ppermute | solution.py:385
  14.1 2.0 %collective-permute-start.5 = (f32[9,16,128]{2,1,0:T(8,128)S(1)}, f32[9,16,128]{2,1,0:T(8,128)S(1)}, u32[]{:S(2)}, u32[]{:S(2)}) collective-permute-start(f32[9,16,128]{2,1,0:T(8,128)S(1)} %get-tuple-element.29), channel_id=1, source_target_pairs={{1,2},{2,1},{5,6},{6,5},{9,10},{10,9},{13,14},{14,13},{17,18},{18,... | collective-permute-start | bytes 221192 | tf_op jit(solution)/shard_map/ppermute | solution.py:385
  16.1 34.3 %all-to-all-start = ((f32[256,1,128]{2,1,0:T(1,128)}), f32[256,1,128]{2,1,0:T(1,128)S(1)}, u32[]{:S(2)}, u32[]{:S(2)}) async-start(f32[256,1,128]{2,1,0:T(1,128)} %bitcast.4), calls=%async_computation | async-start | bytes 262144 | tf_op jit(solution)/shard_map/all_to_all | solution.py:418
  55.9 8.4 %collective-permute-start.6 = (f32[6,4,128]{2,1,0:T(4,128)S(1)}, f32[6,4,128]{2,1,0:T(4,128)S(1)}, u32[]{:S(2)}, u32[]{:S(2)}) collective-permute-start(f32[6,4,128]{2,1,0:T(4,128)S(1)} %get-tuple-element.39), channel_id=1, source_target_pairs={{0,16},{32,48},{64,80},{96,112},{128,144},{160,176},{192,208},{224... | collective-permute-start | bytes 36872 | tf_op jit(solution)/shard_map/ppermute | solution.py:385
  56.3 11.0 %collective-permute-start.7 = (f32[6,4,128]{2,1,0:T(4,128)S(1)}, f32[6,4,128]{2,1,0:T(4,128)S(1)}, u32[]{:S(2)}, u32[]{:S(2)}) collective-permute-start(f32[6,4,128]{2,1,0:T(4,128)S(1)} %get-tuple-element.40), channel_id=1, source_target_pairs={{16,32},{48,64},{80,96},{112,128},{144,160},{176,192},{208,224},{3... | collective-permute-start | bytes 36872 | tf_op jit(solution)/shard_map/ppermute | solution.py:385

commit v4 on v3

--- a/solution.py
+++ b/solution.py
@@ -16,6 +16,7 @@
 BF16 = jnp.bfloat16
 LANES = 128
 DEPTH = 64
+STEP_CELLS = 16
 CELLS = 64
 FACE = 16
 SOURCES = CELLS + 6 * FACE
@@ -261,9 +262,8 @@
     lax.fori_loop(0, CELLS // together, step, 0)
 
 
-def node_kernel(
-    gathered, near, masked, lines, stress, connect, node_pos, drag, fields, first, second,
-    values, sums,
+def force_kernel(
+    gathered, near, masked, lines, stress, connect, node_pos, drag, values, first, second
 ):
     index_x, index_y, index_z = (lax.axis_index(a) for a in AXES)
     device = lax.broadcasted_iota(jnp.int32, (CELLS, 256), 1)
@@ -301,15 +301,55 @@
         high, rest = split2(0.5 * force)
         values[a] = high
         values[3 + a] = rest
+    rows_high = lax.broadcasted_iota(jnp.int32, (8, LANES), 0)
+    rows_low = lax.broadcasted_iota(jnp.int32, (LANES, LANES), 0)
+
+    def scatter(i, total):
+        left, right = [], []
+        for u in range(STEP_CELLS):
+            at = i * STEP_CELLS + u
+            for end in range(2):
+                node = connect[end, pl.ds(at, 1), :]
+                high = node >> 7
+                high = jnp.where(high < 4, high, high - 56)
+                high = jnp.where((node < 512) | (node >= 7680), high, -1)
+                chosen = rows_high == high
+                left.append(
+                    jnp.concatenate(
+                        [jnp.where(chosen, values[q, pl.ds(at, 1), :], 0.0) for q in range(6)],
+                        axis=0,
+                    ).astype(BF16)
+                )
+                right.append((rows_low == (node & 127)).astype(F32).astype(BF16))
+        return total + lax.dot_general(
+            jnp.concatenate(left, axis=1),
+            jnp.concatenate(right, axis=1),
+            (((1,), (1,)), ((), ())),
+            preferred_element_type=F32,
+        )
+
+    total = lax.fori_loop(0, CELLS // STEP_CELLS, scatter, jnp.zeros((48, LANES), F32))
+    even = index_x % 2 == 0
+    for a in range(3):
+        force = total[8 * a : 8 * a + 8] + total[24 + 8 * a : 32 + 8 * a]
+        slow = jnp.concatenate([drag[pl.ds(0, 4), :], drag[pl.ds(60, 4), :]], axis=0)
+        place = jnp.concatenate([node_pos[a, pl.ds(0, 4), :], node_pos[a, pl.ds(60, 4), :]], axis=0)
+        velocity = force / slow
+        for row, field in ((a, place + TIME_STEP * velocity), (3 + a, velocity)):
+            head, tail = field[0:4], field[4:8]
+            first[row] = jnp.where(even, tail, head)
+            second[row] = jnp.where(even, head, tail)
+
+
+def node_kernel(values, connect, node_pos, drag, fields, sums):
     sums[...] = jnp.zeros(sums.shape, F32)
     rows_high = lax.broadcasted_iota(jnp.int32, (32, LANES), 0)
     rows_low = lax.broadcasted_iota(jnp.int32, (256, LANES), 0)
-    step_cells = 16
 
     def scatter(i, carry):
         left, right = [], []
-        for u in range(step_cells):
-            at = i * step_cells + u
+        for u in range(STEP_CELLS):
+            at = i * STEP_CELLS + u
             for end in range(2):
                 node = connect[end, pl.ds(at, 1), :]
                 chosen = rows_high == (node >> 8)
@@ -328,7 +368,7 @@
         )
         return carry
 
-    lax.fori_loop(0, CELLS // step_cells, scatter, 0, unroll=1)
+    lax.fori_loop(0, CELLS // STEP_CELLS, scatter, 0, unroll=1)
     for a in range(3):
         force = sums[pl.ds(32 * a, 32), :] + sums[pl.ds(96 + 32 * a, 32), :]
         fields[3 + a, pl.ds(0, 32, stride=2), :] = force[:, :LANES]
@@ -337,12 +377,6 @@
         velocity = fields[3 + a] / drag[...]
         fields[3 + a] = velocity
         fields[a] = node_pos[a] + TIME_STEP * velocity
-    even = index_x % 2 == 0
-    for a in range(6):
-        tail = fields[a, pl.ds(60, 4), :]
-        head = fields[a, pl.ds(0, 4), :]
-        first[a] = jnp.where(even, tail, head)
-        second[a] = jnp.where(even, head, tail)
 
 
 def migrate_kernel(fields, first, second, shifts, out, joined):
@@ -431,19 +465,23 @@
         compiler_params=params,
         name="near",
     )(offsets, on_chip(masked), lines, *[on_chip(face) for face in received])
-    fields, *ends = pl.pallas_call(
-        node_kernel,
+    values, *ends = pl.pallas_call(
+        force_kernel,
         in_specs=[vmem] * 4 + [smem] + [vmem] * 3,
-        out_shape=[shape(6, 64, LANES), shape(6, 4, LANES), shape(6, 4, LANES)],
-        scratch_shapes=[
-            pltpu.VMEM((6, CELLS, LANES), F32),
-            pltpu.VMEM((192, 256), F32),
-        ],
+        out_shape=[shape(6, CELLS, LANES), shape(6, 4, LANES), shape(6, 4, LANES)],
         compiler_params=params,
-        name="nodes",
+        name="forces",
     )(on_chip(gathered), on_chip(near), on_chip(masked), lines, stress, connect, node_pos, drag)
     second = exchanged(ends[1], "gx", 1)
     first = exchanged(ends[0], "gx", 0)
+    fields = pl.pallas_call(
+        node_kernel,
+        in_specs=[vmem] * 4,
+        out_shape=shape(6, 64, LANES),
+        scratch_shapes=[pltpu.VMEM((192, 256), F32)],
+        compiler_params=params,
+        name="nodes",
+    )(on_chip(values), connect, node_pos, drag)
     out = pl.pallas_call(
         migrate_kernel,
         in_specs=[vmem] * 3 + [smem],

time: 69.8 us -> 69.5 us (level)
  waiting for transfers between devices: 4.42 us -> 1.34 us
  Pallas kernels: 28.8 us -> 31.6 us
    ppermute x8, waiting for transfers between devices: 4.42 us -> 1.34 us  [exchanged(): return lax.ppermute(array, axis, pairs + [(b, a) for a, b in pairs])]
    pallas_call x1 -> x2, Pallas kernels: 5.45 us -> 8.24 us  [the longest x1 4.31 us: shards(): pl.pallas_call(node_kernel, in_specs=[vmem] * 4, out_shape=shape(6, 64, L...]
  transfers between devices with their start and end apart: 9 -> 9, of which waited for: 4 -> 3; matrix products, arithmetic and copies ran while one was open for 0% -> 0% of each run, Pallas kernels for 27% -> 34%
where the time goes in v4:
time: 69.5 us; the launch traced here: 69.1 us
  starting transfers between devices  36.1 us (52%)
  Pallas kernels  31.6 us (45%)
  waiting for transfers between devices  1.34 us (2%)
    ppermute x8, starting transfers between devices, exchanged(): return lax.ppermute(array, axis, pairs + [(b, a) for a, b in pairs])  20.8 us
    pallas_call x1, Pallas kernels, shards(): pl.pallas_call(near_kernel, in_specs=[vmem] * 9, out_shape=shape(CELLS, 3...  19 us
    all_to_all x1, starting transfers between devices, shards(): lax.all_to_all(moments.reshape(256, 1, LANES), AXES, 0, 0, tiled=True)  15.3 us
    pallas_call x1, Pallas kernels, shards(): pl.pallas_call(node_kernel, in_specs=[vmem] * 4, out_shape=shape(6, 64, L...  4.31 us
    pallas_call x1, Pallas kernels, shards(): pl.pallas_call(force_kernel, in_specs=[vmem] * 4 + [smem] + [vmem] * 3, o...  3.93 us
    pallas_call x1, Pallas kernels, shards(): pl.pallas_call(prepare_kernel, in_specs=[vmem, vmem, vmem, smem], out_sha...  2.27 us
    pallas_call x1, Pallas kernels, shards(): pl.pallas_call(migrate_kernel, in_specs=[vmem] * 3 + [smem], out_shape=ja...  2.07 us
  transfers between devices with their start and end apart: 9, of which 3 were waited for; matrix products, arithmetic and copies ran while one was open for 0% of the time, Pallas kernels for 34%

profile of v4, /device:TPU:25, one launch (start us, length us, event | category | flops | bytes accessed | tf_op | source)
XLA Modules:
  0.0 69.1 jit_solution(15946641004052117973)
XLA Ops:
  0.0 2.3 %prepare.1 = (f32[3,64,128]{2,1,0:T(8,128)S(1)}, f32[256,128]{1,0:T(8,128)}, f32[9,16,128]{2,1,0:T(8,128)S(1)}, f32[9,16,128]{2,1,0:T(8,128)S(1)}, f32[9,16,128]...) custom-call(f32[3,64,128]{2,1,0:T(8,128)} %bitcast.18, ...), custom_call_target="tpu_custom_call" | custom-call | tf_op jit(solution)/shard_map/prepare/pallas_call | solution.py:441
  2.3 0.7 collective-permute-start
  2.9 8.4 %collective-permute-start.1 = (f32[9,16,128]{2,1,0:T(8,128)S(1)}, f32[9,16,128]{2,1,0:T(8,128)S(1)}, u32[]{:S(2)}, u32[]{:S(2)}) collective-permute-start(f32[9,16,128]{2,1,0:T(8,128)S(1)} %get-tuple-element.25), channel_id=1, source_target_pairs={{16,32},{48,64},{80,96},{112,128},{144,160},{176,192},{208,224},{3... | collective-permute-start | bytes 221192 | tf_op jit(solution)/shard_map/ppermute | solution.py:419
  11.3 0.8 %collective-permute-start.2 = (f32[9,16,128]{2,1,0:T(8,128)S(1)}, f32[9,16,128]{2,1,0:T(8,128)S(1)}, u32[]{:S(2)}, u32[]{:S(2)}) collective-permute-start(f32[9,16,128]{2,1,0:T(8,128)S(1)} %get-tuple-element.26), channel_id=1, source_target_pairs={{0,4},{8,12},{4,0},{12,8},{1,5},{9,13},{5,1},{13,9},{2,6},{10,14},... | collective-permute-start | bytes 221192 | tf_op jit(solution)/shard_map/ppermute | solution.py:419
  12.1 0.7 collective-permute-start.3
  12.8 1.3 %collective-permute-start.4 = (f32[9,16,128]{2,1,0:T(8,128)S(1)}, f32[9,16,128]{2,1,0:T(8,128)S(1)}, u32[]{:S(2)}, u32[]{:S(2)}) collective-permute-start(f32[9,16,128]{2,1,0:T(8,128)S(1)} %get-tuple-element.28), channel_id=1, source_target_pairs={{0,1},{2,3},{1,0},{3,2},{4,5},{6,7},{5,4},{7,6},{8,9},{10,11},{9,8... | collective-permute-start | bytes 221192 | tf_op jit(solution)/shard_map/ppermute | solution.py:419
  14.1 0.0 collective-permute-done.refs_3_
  14.1 0.7 collective-permute-start.5
  14.8 0.2 collective-permute-done.1.refs_4_
  14.9 0.5 collective-permute-done.2.refs_5_
  15.4 0.0 collective-permute-done.3.refs_6_
  15.4 0.7 %collective-permute-done.4.refs_7_ = f32[9,16,128]{2,1,0:T(8,128)S(1)} collective-permute-done((f32[9,16,128]{2,1,0:T(8,128)S(1)}, f32[9,16,128]{2,1,0:T(8,128)S(1)}, u32[]{:S(2)}, u32[]{:S(2)}) %collective-permute-start.4) | collective-permute-done | bytes 73760 | tf_op jit(solution)/shard_map/ppermute | solution.py:419
  16.1 0.0 collective-permute-done.5.refs_8_
  16.1 15.3 %all-to-all-start = ((f32[256,1,128]{2,1,0:T(1,128)}), f32[256,1,128]{2,1,0:T(1,128)S(1)}, u32[]{:S(2)}, u32[]{:S(2)}) async-start(f32[256,1,128]{2,1,0:T(1,128)} %bitcast.4), calls=%async_computation | async-start | bytes 262144 | tf_op jit(solution)/shard_map/all_to_all | solution.py:452
  31.4 19.0 %near.1 = f32[64,3,128]{2,1,0:T(4,128)S(1)} custom-call(f32[3,64,128]{2,1,0:T(8,128)} %bitcast.19, f32[3,64,128]{2,1,0:T(8,128)S(1)} %get-tuple-element.31.refs_1_.masked, f32[3,64,128]{2,1,0:T(8,128)} %bitcast.14, f32[9,16,128]{2,1,0:T(8,128)S(1)} %collective-permute-done.refs_3_, f32[9,16,128]{2,1,0:T(8,128)S(1)} %collective-permute-done.1.refs_4_, ...), custom_call_target="tpu_custom_call" | custom-call | tf_op jit(solution)/shard_map/near/pallas_call | solution.py:455
  50.4 0.0 all-to-all-done
  50.4 3.9 %forces.1 = (f32[6,64,128]{2,1,0:T(8,128)S(1)}, f32[6,4,128]{2,1,0:T(4,128)S(1)}, f32[6,4,128]{2,1,0:T(4,128)S(1)}) custom-call(f32[256,128]{1,0:T(8,128)S(1)} %bitcast.12, f32[64,3,128]{2,1,0:T(4,128)S(1)} %near.1, f32[3,64,128]{2,1,0:T(8,128)S(1)} %get-tuple-element.31.refs_1_.masked, f32[3,64,128]{2,1,0:T(8,128)} %bitcast.15, f32[3,3]{1,0:T(4,128)} %stress.1, ...), custom_call_target="tpu_custom_call" | custom-call | tf_op jit(solution)/shard_map/forces/pallas_call | solution.py:468
  54.4 0.4 collective-permute-start.6
  54.8 7.9 %collective-permute-start.7 = (f32[6,4,128]{2,1,0:T(4,128)S(1)}, f32[6,4,128]{2,1,0:T(4,128)S(1)}, u32[]{:S(2)}, u32[]{:S(2)}) collective-permute-start(f32[6,4,128]{2,1,0:T(4,128)S(1)} %get-tuple-element.40), channel_id=1, source_target_pairs={{16,32},{48,64},{80,96},{112,128},{144,160},{176,192},{208,224},{3... | collective-permute-start | bytes 36872 | tf_op jit(solution)/shard_map/ppermute | solution.py:419
  62.7 4.3 %nodes.1.fields = f32[6,64,128]{2,1,0:T(8,128)S(1)} custom-call(f32[6,64,128]{2,1,0:T(8,128)S(1)} %get-tuple-element.38.values, s32[2,64,128]{2,1,0:T(8,128)} %bitcast.21, f32[3,64,128]{2,1,0:T(8,128)} %bitcast.17, f32[64,128]{1,0:T(8,128)} %bitcast.23), custom_call_target="tpu_custom_call" | custom-call | tf_op jit(solution)/shard_map/nodes/pallas_call | solution.py:477
  67.1 0.0 collective-permute-done.6.first
  67.1 0.0 collective-permute-done.7.second
  67.1 2.1 %migrate.1 = f32[6,72,128]{2,1,0:T(8,128)} custom-call(f32[6,64,128]{2,1,0:T(8,128)S(1)} %nodes.1.fields, f32[6,4,128]{2,1,0:T(4,128)S(1)} %collective-permute-done.6.first, f32[6,4,128]{2,1,0:T(4,128)S(1)} %collective-permute-done.7.second, s32[2,4,4,16]{3,2,1,0:T(4,128)} %bitcast.25), custom_call_target="tpu_custom_call" | custom-call | tf_op jit(solution)/shard_map/migrate/pallas_call | solution.py:485
Async XLA Ops:
  2.3 11.8 %collective-permute-start = (f32[9,16,128]{2,1,0:T(8,128)S(1)}, f32[9,16,128]{2,1,0:T(8,128)S(1)}, u32[]{:S(2)}, u32[]{:S(2)}) collective-permute-start(f32[9,16,128]{2,1,0:T(8,128)S(1)} %get-tuple-element.24), channel_id=1, source_target_pairs={{0,16},{32,48},{64,80},{96,112},{128,144},{160,176},{192,208},{224... | collective-permute-start | bytes 221192 | tf_op jit(solution)/shard_map/ppermute | solution.py:419
  2.9 12.0 %collective-permute-start.1 = (f32[9,16,128]{2,1,0:T(8,128)S(1)}, f32[9,16,128]{2,1,0:T(8,128)S(1)}, u32[]{:S(2)}, u32[]{:S(2)}) collective-permute-start(f32[9,16,128]{2,1,0:T(8,128)S(1)} %get-tuple-element.25), channel_id=1, source_target_pairs={{16,32},{48,64},{80,96},{112,128},{144,160},{176,192},{208,224},{3... | collective-permute-start | bytes 221192 | tf_op jit(solution)/shard_map/ppermute | solution.py:419
  11.3 4.1 %collective-permute-start.2 = (f32[9,16,128]{2,1,0:T(8,128)S(1)}, f32[9,16,128]{2,1,0:T(8,128)S(1)}, u32[]{:S(2)}, u32[]{:S(2)}) collective-permute-start(f32[9,16,128]{2,1,0:T(8,128)S(1)} %get-tuple-element.26), channel_id=1, source_target_pairs={{0,4},{8,12},{4,0},{12,8},{1,5},{9,13},{5,1},{13,9},{2,6},{10,14},... | collective-permute-start | bytes 221192 | tf_op jit(solution)/shard_map/ppermute | solution.py:419
  12.1 3.3 %collective-permute-start.3 = (f32[9,16,128]{2,1,0:T(8,128)S(1)}, f32[9,16,128]{2,1,0:T(8,128)S(1)}, u32[]{:S(2)}, u32[]{:S(2)}) collective-permute-start(f32[9,16,128]{2,1,0:T(8,128)S(1)} %get-tuple-element.27), channel_id=1, source_target_pairs={{4,8},{8,4},{5,9},{9,5},{6,10},{10,6},{7,11},{11,7},{20,24},{24,20... | collective-permute-start | bytes 221192 | tf_op jit(solution)/shard_map/ppermute | solution.py:419
  12.8 3.3 %collective-permute-start.4 = (f32[9,16,128]{2,1,0:T(8,128)S(1)}, f32[9,16,128]{2,1,0:T(8,128)S(1)}, u32[]{:S(2)}, u32[]{:S(2)}) collective-permute-start(f32[9,16,128]{2,1,0:T(8,128)S(1)} %get-tuple-element.28), channel_id=1, source_target_pairs={{0,1},{2,3},{1,0},{3,2},{4,5},{6,7},{5,4},{7,6},{8,9},{10,11},{9,8... | collective-permute-start | bytes 221192 | tf_op jit(solution)/shard_map/ppermute | solution.py:419
  14.1 2.0 %collective-permute-start.5 = (f32[9,16,128]{2,1,0:T(8,128)S(1)}, f32[9,16,128]{2,1,0:T(8,128)S(1)}, u32[]{:S(2)}, u32[]{:S(2)}) collective-permute-start(f32[9,16,128]{2,1,0:T(8,128)S(1)} %get-tuple-element.29), channel_id=1, source_target_pairs={{1,2},{2,1},{5,6},{6,5},{9,10},{10,9},{13,14},{14,13},{17,18},{18,... | collective-permute-start | bytes 221192 | tf_op jit(solution)/shard_map/ppermute | solution.py:419
  16.1 34.3 %all-to-all-start = ((f32[256,1,128]{2,1,0:T(1,128)}), f32[256,1,128]{2,1,0:T(1,128)S(1)}, u32[]{:S(2)}, u32[]{:S(2)}) async-start(f32[256,1,128]{2,1,0:T(1,128)} %bitcast.4), calls=%async_computation | async-start | bytes 262144 | tf_op jit(solution)/shard_map/all_to_all | solution.py:452
  54.4 12.7 %collective-permute-start.6 = (f32[6,4,128]{2,1,0:T(4,128)S(1)}, f32[6,4,128]{2,1,0:T(4,128)S(1)}, u32[]{:S(2)}, u32[]{:S(2)}) collective-permute-start(f32[6,4,128]{2,1,0:T(4,128)S(1)} %get-tuple-element.39), channel_id=1, source_target_pairs={{0,16},{32,48},{64,80},{96,112},{128,144},{160,176},{192,208},{224... | collective-permute-start | bytes 36872 | tf_op jit(solution)/shard_map/ppermute | solution.py:419
  54.8 12.3 %collective-permute-start.7 = (f32[6,4,128]{2,1,0:T(4,128)S(1)}, f32[6,4,128]{2,1,0:T(4,128)S(1)}, u32[]{:S(2)}, u32[]{:S(2)}) collective-permute-start(f32[6,4,128]{2,1,0:T(4,128)S(1)} %get-tuple-element.40), channel_id=1, source_target_pairs={{16,32},{48,64},{80,96},{112,128},{144,160},{176,192},{208,224},{3... | collective-permute-start | bytes 36872 | tf_op jit(solution)/shard_map/ppermute | solution.py:419

commit v5 on v4

--- a/solution.py
+++ b/solution.py
@@ -17,6 +17,7 @@
 LANES = 128
 DEPTH = 64
 STEP_CELLS = 16
+ORDER = (1, 3, 5, 2, 4, 0)
 CELLS = 64
 FACE = 16
 SOURCES = CELLS + 6 * FACE
@@ -54,6 +55,7 @@
         for axis in range(3):
             block = burgers[axis, pl.ds(8 * group, 8), :]
             masked[axis, pl.ds(8 * group, 8), :] = jnp.where(slot < live, block, 0.0)
+    sends = [sends[ORDER.index(i)] for i in range(6)]
     for axis in range(3):
         even = lax.axis_index(AXES[axis]) % 2 == 0
         to = 0
@@ -263,7 +265,7 @@
 
 
 def force_kernel(
-    gathered, near, masked, lines, stress, connect, node_pos, drag, values, first, second
+    gathered, near, masked, lines, stress, connect, node_pos, drag, values, second, first
 ):
     index_x, index_y, index_z = (lax.axis_index(a) for a in AXES)
     device = lax.broadcasted_iota(jnp.int32, (CELLS, 256), 1)
@@ -446,9 +448,11 @@
         name="prepare",
     )(offsets, burgers, lines, counts)
     received = [None] * 6
-    for i in (1, 3, 5, 0, 2, 4):
-        received[i] = exchanged(sends[i], AXES[i // 2], i % 2)
-    moments, *received = lax.optimization_barrier((moments, *received))
+    for i, send in zip(ORDER, sends):
+        received[i] = exchanged(send, AXES[i // 2], i % 2)
+    moments, *early = lax.optimization_barrier((moments, *[received[i] for i in ORDER[:5]]))
+    for i, face in zip(ORDER, early):
+        received[i] = face
     gathered = lax.all_to_all(
         moments.reshape(256, 1, LANES), AXES, 0, 0, tiled=True
     ).reshape(256, LANES)
@@ -472,8 +476,8 @@
         compiler_params=params,
         name="forces",
     )(on_chip(gathered), on_chip(near), on_chip(masked), lines, stress, connect, node_pos, drag)
-    second = exchanged(ends[1], "gx", 1)
-    first = exchanged(ends[0], "gx", 0)
+    second = exchanged(ends[0], "gx", 1)
+    first = exchanged(ends[1], "gx", 0)
     fields = pl.pallas_call(
         node_kernel,
         in_specs=[vmem] * 4,

time: 69.5 us -> 69.6 us (level)
  waiting for transfers between devices: 1.34 us -> 2.65 us
  starting transfers between devices: 36.1 us -> 34.9 us
    all_to_all x1, starting transfers between devices: 15.3 us -> 9.28 us  [shards(): lax.all_to_all(moments.reshape(256, 1, LANES), AXES, 0, 0, tiled=True)]
    ppermute x8, starting transfers between devices: 20.8 us -> 25.6 us  [exchanged(): return lax.ppermute(array, axis, pairs + [(b, a) for a, b in pairs])]
    ppermute x8, waiting for transfers between devices: 1.34 us -> 2.65 us  [exchanged(): return lax.ppermute(array, axis, pairs + [(b, a) for a, b in pairs])]
  transfers between devices with their start and end apart: 9 -> 9, of which waited for: 3 -> 2; matrix products, arithmetic and copies ran while one was open for 0% -> 0% of each run, Pallas kernels for 34% -> 34%
where the time goes in v5:
time: 69.6 us; the launch traced here: 69.2 us
  starting transfers between devices  34.9 us (50%)
  Pallas kernels  31.6 us (45%)
  waiting for transfers between devices  2.65 us (4%)
    ppermute x8, starting transfers between devices, exchanged(): return lax.ppermute(array, axis, pairs + [(b, a) for a, b in pairs])  25.6 us
    pallas_call x1, Pallas kernels, shards(): pl.pallas_call(near_kernel, in_specs=[vmem] * 9, out_shape=shape(CELLS, 3...  19 us
    all_to_all x1, starting transfers between devices, shards(): lax.all_to_all(moments.reshape(256, 1, LANES), AXES, 0, 0, tiled=True)  9.28 us
    pallas_call x1, Pallas kernels, shards(): pl.pallas_call(node_kernel, in_specs=[vmem] * 4, out_shape=shape(6, 64, L...  4.31 us
    pallas_call x1, Pallas kernels, shards(): pl.pallas_call(force_kernel, in_specs=[vmem] * 4 + [smem] + [vmem] * 3, o...  3.93 us
    ppermute x8, waiting for transfers between devices, exchanged(): return lax.ppermute(array, axis, pairs + [(b, a) for a, b in pairs])  2.65 us
    pallas_call x1, Pallas kernels, shards(): pl.pallas_call(prepare_kernel, in_specs=[vmem, vmem, vmem, smem], out_sha...  2.27 us
    pallas_call x1, Pallas kernels, shards(): pl.pallas_call(migrate_kernel, in_specs=[vmem] * 3 + [smem], out_shape=ja...  2.06 us
  transfers between devices with their start and end apart: 9, of which 2 were waited for; matrix products, arithmetic and copies ran while one was open for 0% of the time, Pallas kernels for 34%

profile of v5, /device:TPU:25, one launch (start us, length us, event | category | flops | bytes accessed | tf_op | source)
XLA Modules:
  0.0 69.2 jit_solution(15498670569839351694)
XLA Ops:
  0.0 2.3 %prepare.1 = (f32[3,64,128]{2,1,0:T(8,128)S(1)}, f32[256,128]{1,0:T(8,128)}, f32[9,16,128]{2,1,0:T(8,128)S(1)}, f32[9,16,128]{2,1,0:T(8,128)S(1)}, f32[9,16,128]...) custom-call(f32[3,64,128]{2,1,0:T(8,128)} %bitcast.18, ...), custom_call_target="tpu_custom_call" | custom-call | tf_op jit(solution)/shard_map/prepare/pallas_call | solution.py:443
  2.3 9.0 %collective-permute-start = (f32[9,16,128]{2,1,0:T(8,128)S(1)}, f32[9,16,128]{2,1,0:T(8,128)S(1)}, u32[]{:S(2)}, u32[]{:S(2)}) collective-permute-start(f32[9,16,128]{2,1,0:T(8,128)S(1)} %get-tuple-element.23), channel_id=1, source_target_pairs={{16,32},{48,64},{80,96},{112,128},{144,160},{176,192},{208,224},{3... | collective-permute-start | bytes 221192 | tf_op jit(solution)/shard_map/ppermute | solution.py:421
  11.3 0.7 collective-permute-start.1
  12.0 0.7 collective-permute-start.2
  12.7 2.8 %collective-permute-start.3 = (f32[9,16,128]{2,1,0:T(8,128)S(1)}, f32[9,16,128]{2,1,0:T(8,128)S(1)}, u32[]{:S(2)}, u32[]{:S(2)}) collective-permute-start(f32[9,16,128]{2,1,0:T(8,128)S(1)} %get-tuple-element.26), channel_id=1, source_target_pairs={{0,4},{8,12},{4,0},{12,8},{1,5},{9,13},{5,1},{13,9},{2,6},{10,14},... | collective-permute-start | bytes 221192 | tf_op jit(solution)/shard_map/ppermute | solution.py:421
  15.5 3.7 %collective-permute-start.4 = (f32[9,16,128]{2,1,0:T(8,128)S(1)}, f32[9,16,128]{2,1,0:T(8,128)S(1)}, u32[]{:S(2)}, u32[]{:S(2)}) collective-permute-start(f32[9,16,128]{2,1,0:T(8,128)S(1)} %get-tuple-element.27), channel_id=1, source_target_pairs={{0,1},{2,3},{1,0},{3,2},{4,5},{6,7},{5,4},{7,6},{8,9},{10,11},{9,8... | collective-permute-start | bytes 221192 | tf_op jit(solution)/shard_map/ppermute | solution.py:421
  19.1 0.0 collective-permute-done.refs_4_
  19.1 0.0 collective-permute-done.1.refs_6_
  19.1 0.0 collective-permute-done.2.refs_8_
  19.1 0.0 collective-permute-done.3.refs_5_
  19.1 1.7 %collective-permute-done.4.refs_7_ = f32[9,16,128]{2,1,0:T(8,128)S(1)} collective-permute-done((f32[9,16,128]{2,1,0:T(8,128)S(1)}, f32[9,16,128]{2,1,0:T(8,128)S(1)}, u32[]{:S(2)}, u32[]{:S(2)}) %collective-permute-start.4) | collective-permute-done | bytes 73760 | tf_op jit(solution)/shard_map/ppermute | solution.py:421
  20.9 9.3 %all-to-all-start = ((f32[256,1,128]{2,1,0:T(1,128)}), f32[256,1,128]{2,1,0:T(1,128)S(1)}, u32[]{:S(2)}, u32[]{:S(2)}) async-start(f32[256,1,128]{2,1,0:T(1,128)} %bitcast.4), calls=%async_computation | async-start | bytes 262144 | tf_op jit(solution)/shard_map/all_to_all | solution.py:456
  30.2 0.4 collective-permute-start.5
  30.6 0.9 %collective-permute-done.5.refs_3_ = f32[9,16,128]{2,1,0:T(8,128)S(1)} collective-permute-done((f32[9,16,128]{2,1,0:T(8,128)S(1)}, f32[9,16,128]{2,1,0:T(8,128)S(1)}, u32[]{:S(2)}, u32[]{:S(2)}) %collective-permute-start.5) | collective-permute-done | bytes 73760 | tf_op jit(solution)/shard_map/ppermute | solution.py:421
  31.5 19.0 %near.1 = f32[64,3,128]{2,1,0:T(4,128)S(1)} custom-call(f32[3,64,128]{2,1,0:T(8,128)} %bitcast.19, f32[3,64,128]{2,1,0:T(8,128)S(1)} %get-tuple-element.29.refs_1_.masked, f32[3,64,128]{2,1,0:T(8,128)} %bitcast.14, f32[9,16,128]{2,1,0:T(8,128)S(1)} %collective-permute-done.5.refs_3_, f32[9,16,128]{2,1,0:T(8,128)S(1)} %collective-permute-done.refs_4_, ...), custom_call_target="tpu_custom_call" | custom-call | tf_op jit(solution)/shard_map/near/pallas_call | solution.py:459
  50.5 0.0 all-to-all-done
  50.5 3.9 %forces.1 = (f32[6,64,128]{2,1,0:T(8,128)S(1)}, f32[6,4,128]{2,1,0:T(4,128)S(1)}, f32[6,4,128]{2,1,0:T(4,128)S(1)}) custom-call(f32[256,128]{1,0:T(8,128)S(1)} %bitcast.12, f32[64,3,128]{2,1,0:T(4,128)S(1)} %near.1, f32[3,64,128]{2,1,0:T(8,128)S(1)} %get-tuple-element.29.refs_1_.masked, f32[3,64,128]{2,1,0:T(8,128)} %bitcast.15, f32[3,3]{1,0:T(4,128)} %stress.1, ...), custom_call_target="tpu_custom_call" | custom-call | tf_op jit(solution)/shard_map/forces/pallas_call | solution.py:472
  54.5 0.4 collective-permute-start.6
  54.9 7.9 %collective-permute-start.7 = (f32[6,4,128]{2,1,0:T(4,128)S(1)}, f32[6,4,128]{2,1,0:T(4,128)S(1)}, u32[]{:S(2)}, u32[]{:S(2)}) collective-permute-start(f32[6,4,128]{2,1,0:T(4,128)S(1)} %get-tuple-element.38), channel_id=1, source_target_pairs={{16,32},{48,64},{80,96},{112,128},{144,160},{176,192},{208,224},{3... | collective-permute-start | bytes 36872 | tf_op jit(solution)/shard_map/ppermute | solution.py:421
  62.8 4.3 %nodes.1.fields = f32[6,64,128]{2,1,0:T(8,128)S(1)} custom-call(f32[6,64,128]{2,1,0:T(8,128)S(1)} %get-tuple-element.36.values, s32[2,64,128]{2,1,0:T(8,128)} %bitcast.21, f32[3,64,128]{2,1,0:T(8,128)} %bitcast.17, f32[64,128]{1,0:T(8,128)} %bitcast.23), custom_call_target="tpu_custom_call" | custom-call | tf_op jit(solution)/shard_map/nodes/pallas_call | solution.py:481
  67.1 0.0 collective-permute-done.6.first
  67.1 0.0 collective-permute-done.7.second
  67.2 2.1 %migrate.1 = f32[6,72,128]{2,1,0:T(8,128)} custom-call(f32[6,64,128]{2,1,0:T(8,128)S(1)} %nodes.1.fields, f32[6,4,128]{2,1,0:T(4,128)S(1)} %collective-permute-done.6.first, f32[6,4,128]{2,1,0:T(4,128)S(1)} %collective-permute-done.7.second, s32[2,4,4,16]{3,2,1,0:T(4,128)} %bitcast.25), custom_call_target="tpu_custom_call" | custom-call | tf_op jit(solution)/shard_map/migrate/pallas_call | solution.py:489
Async XLA Ops:
  2.3 16.9 %collective-permute-start = (f32[9,16,128]{2,1,0:T(8,128)S(1)}, f32[9,16,128]{2,1,0:T(8,128)S(1)}, u32[]{:S(2)}, u32[]{:S(2)}) collective-permute-start(f32[9,16,128]{2,1,0:T(8,128)S(1)} %get-tuple-element.23), channel_id=1, source_target_pairs={{16,32},{48,64},{80,96},{112,128},{144,160},{176,192},{208,224},{3... | collective-permute-start | bytes 221192 | tf_op jit(solution)/shard_map/ppermute | solution.py:421
  11.3 7.8 %collective-permute-start.1 = (f32[9,16,128]{2,1,0:T(8,128)S(1)}, f32[9,16,128]{2,1,0:T(8,128)S(1)}, u32[]{:S(2)}, u32[]{:S(2)}) collective-permute-start(f32[9,16,128]{2,1,0:T(8,128)S(1)} %get-tuple-element.24), channel_id=1, source_target_pairs={{4,8},{8,4},{5,9},{9,5},{6,10},{10,6},{7,11},{11,7},{20,24},{24,20... | collective-permute-start | bytes 221192 | tf_op jit(solution)/shard_map/ppermute | solution.py:421
  12.0 7.2 %collective-permute-start.2 = (f32[9,16,128]{2,1,0:T(8,128)S(1)}, f32[9,16,128]{2,1,0:T(8,128)S(1)}, u32[]{:S(2)}, u32[]{:S(2)}) collective-permute-start(f32[9,16,128]{2,1,0:T(8,128)S(1)} %get-tuple-element.25), channel_id=1, source_target_pairs={{1,2},{2,1},{5,6},{6,5},{9,10},{10,9},{13,14},{14,13},{17,18},{18,... | collective-permute-start | bytes 221192 | tf_op jit(solution)/shard_map/ppermute | solution.py:421
  12.7 6.5 %collective-permute-start.3 = (f32[9,16,128]{2,1,0:T(8,128)S(1)}, f32[9,16,128]{2,1,0:T(8,128)S(1)}, u32[]{:S(2)}, u32[]{:S(2)}) collective-permute-start(f32[9,16,128]{2,1,0:T(8,128)S(1)} %get-tuple-element.26), channel_id=1, source_target_pairs={{0,4},{8,12},{4,0},{12,8},{1,5},{9,13},{5,1},{13,9},{2,6},{10,14},... | collective-permute-start | bytes 221192 | tf_op jit(solution)/shard_map/ppermute | solution.py:421
  15.5 5.4 %collective-permute-start.4 = (f32[9,16,128]{2,1,0:T(8,128)S(1)}, f32[9,16,128]{2,1,0:T(8,128)S(1)}, u32[]{:S(2)}, u32[]{:S(2)}) collective-permute-start(f32[9,16,128]{2,1,0:T(8,128)S(1)} %get-tuple-element.27), channel_id=1, source_target_pairs={{0,1},{2,3},{1,0},{3,2},{4,5},{6,7},{5,4},{7,6},{8,9},{10,11},{9,8... | collective-permute-start | bytes 221192 | tf_op jit(solution)/shard_map/ppermute | solution.py:421
  20.9 29.6 %all-to-all-start = ((f32[256,1,128]{2,1,0:T(1,128)}), f32[256,1,128]{2,1,0:T(1,128)S(1)}, u32[]{:S(2)}, u32[]{:S(2)}) async-start(f32[256,1,128]{2,1,0:T(1,128)} %bitcast.4), calls=%async_computation | async-start | bytes 262144 | tf_op jit(solution)/shard_map/all_to_all | solution.py:456
  30.2 1.4 %collective-permute-start.5 = (f32[9,16,128]{2,1,0:T(8,128)S(1)}, f32[9,16,128]{2,1,0:T(8,128)S(1)}, u32[]{:S(2)}, u32[]{:S(2)}) collective-permute-start(f32[9,16,128]{2,1,0:T(8,128)S(1)} %get-tuple-element.30), channel_id=1, source_target_pairs={{0,16},{32,48},{64,80},{96,112},{128,144},{160,176},{192,208},{224... | collective-permute-start | bytes 221192 | tf_op jit(solution)/shard_map/ppermute | solution.py:421
  54.5 12.7 %collective-permute-start.6 = (f32[6,4,128]{2,1,0:T(4,128)S(1)}, f32[6,4,128]{2,1,0:T(4,128)S(1)}, u32[]{:S(2)}, u32[]{:S(2)}) collective-permute-start(f32[6,4,128]{2,1,0:T(4,128)S(1)} %get-tuple-element.37), channel_id=1, source_target_pairs={{0,16},{32,48},{64,80},{96,112},{128,144},{160,176},{192,208},{224... | collective-permute-start | bytes 36872 | tf_op jit(solution)/shard_map/ppermute | solution.py:421
  54.9 12.2 %collective-permute-start.7 = (f32[6,4,128]{2,1,0:T(4,128)S(1)}, f32[6,4,128]{2,1,0:T(4,128)S(1)}, u32[]{:S(2)}, u32[]{:S(2)}) collective-permute-start(f32[6,4,128]{2,1,0:T(4,128)S(1)} %get-tuple-element.38), channel_id=1, source_target_pairs={{16,32},{48,64},{80,96},{112,128},{144,160},{176,192},{208,224},{3... | collective-permute-start | bytes 36872 | tf_op jit(solution)/shard_map/ppermute | solution.py:421

commit v6 on v5

--- a/solution.py
+++ b/solution.py
@@ -85,19 +85,20 @@
                     )
                 )
     stack = jnp.concatenate(rows, axis=0)
-    ones = jnp.ones((8, LANES), F32)
+    ones = jnp.ones((8, 3 * LANES), F32).astype(BF16)
     summed = lax.dot_general(
         ones,
-        stack,
+        jnp.concatenate(split3(stack), axis=1).astype(BF16),
         (((1,), (1,)), ((), ())),
-        precision=lax.Precision.HIGHEST,
         preferred_element_type=F32,
     )
     n = lax.broadcasted_iota(jnp.int32, (288, LANES), 0)
     lane = lax.broadcasted_iota(jnp.int32, (288, LANES), 1)
     target = ((n // 72) * 2 + (n % 4) // 2) * 16 + (n // 8) % 9
-    pick = (lane == target).astype(F32)
-    packed = jnp.dot(summed, pick, precision=lax.Precision.HIGHEST, preferred_element_type=F32)
+    pick = (lane == target).astype(F32).astype(BF16)
+    packed = sum(
+        jnp.dot(part.astype(BF16), pick, preferred_element_type=F32) for part in split3(summed)
+    )
     moments[...] = jnp.broadcast_to(packed[0:1], moments.shape)
 
 

time: 69.6 us -> 69.4 us (level)
  no operation moved by 1% of the time
where the time goes in v6:
time: 69.4 us; the launch traced here: 69 us
  starting transfers between devices  34.9 us (50%)
  Pallas kernels  31.4 us (45%)
  waiting for transfers between devices  2.65 us (4%)
    ppermute x8, starting transfers between devices, exchanged(): return lax.ppermute(array, axis, pairs + [(b, a) for a, b in pairs])  25.6 us
    pallas_call x1, Pallas kernels, shards(): pl.pallas_call(near_kernel, in_specs=[vmem] * 9, out_shape=shape(CELLS, 3...  19 us
    all_to_all x1, starting transfers between devices, shards(): lax.all_to_all(moments.reshape(256, 1, LANES), AXES, 0, 0, tiled=True)  9.28 us
    pallas_call x1, Pallas kernels, shards(): pl.pallas_call(node_kernel, in_specs=[vmem] * 4, out_shape=shape(6, 64, L...  4.31 us
    pallas_call x1, Pallas kernels, shards(): pl.pallas_call(force_kernel, in_specs=[vmem] * 4 + [smem] + [vmem] * 3, o...  3.93 us
    ppermute x8, waiting for transfers between devices, exchanged(): return lax.ppermute(array, axis, pairs + [(b, a) for a, b in pairs])  2.65 us
    pallas_call x1, Pallas kernels, shards(): pl.pallas_call(prepare_kernel, in_specs=[vmem, vmem, vmem, smem], out_sha...  2.09 us
    pallas_call x1, Pallas kernels, shards(): pl.pallas_call(migrate_kernel, in_specs=[vmem] * 3 + [smem], out_shape=ja...  2.07 us
  transfers between devices with their start and end apart: 9, of which 2 were waited for; matrix products, arithmetic and copies ran while one was open for 0% of the time, Pallas kernels for 34%

profile of v6, /device:TPU:25, one launch (start us, length us, event | category | flops | bytes accessed | tf_op | source)
XLA Modules:
  0.0 69.0 jit_solution(5904226529131870641)
XLA Ops:
  0.0 2.1 %prepare.1 = (f32[3,64,128]{2,1,0:T(8,128)S(1)}, f32[256,128]{1,0:T(8,128)}, f32[9,16,128]{2,1,0:T(8,128)S(1)}, f32[9,16,128]{2,1,0:T(8,128)S(1)}, f32[9,16,128]...) custom-call(f32[3,64,128]{2,1,0:T(8,128)} %bitcast.18, ...), custom_call_target="tpu_custom_call" | custom-call | tf_op jit(solution)/shard_map/prepare/pallas_call | solution.py:444
  2.1 9.0 %collective-permute-start = (f32[9,16,128]{2,1,0:T(8,128)S(1)}, f32[9,16,128]{2,1,0:T(8,128)S(1)}, u32[]{:S(2)}, u32[]{:S(2)}) collective-permute-start(f32[9,16,128]{2,1,0:T(8,128)S(1)} %get-tuple-element.23), channel_id=1, source_target_pairs={{16,32},{48,64},{80,96},{112,128},{144,160},{176,192},{208,224},{3... | collective-permute-start | bytes 221192 | tf_op jit(solution)/shard_map/ppermute | solution.py:422
  11.1 0.7 collective-permute-start.1
  11.8 0.7 collective-permute-start.2
  12.5 2.8 %collective-permute-start.3 = (f32[9,16,128]{2,1,0:T(8,128)S(1)}, f32[9,16,128]{2,1,0:T(8,128)S(1)}, u32[]{:S(2)}, u32[]{:S(2)}) collective-permute-start(f32[9,16,128]{2,1,0:T(8,128)S(1)} %get-tuple-element.26), channel_id=1, source_target_pairs={{0,4},{8,12},{4,0},{12,8},{1,5},{9,13},{5,1},{13,9},{2,6},{10,14},... | collective-permute-start | bytes 221192 | tf_op jit(solution)/shard_map/ppermute | solution.py:422
  15.3 3.7 %collective-permute-start.4 = (f32[9,16,128]{2,1,0:T(8,128)S(1)}, f32[9,16,128]{2,1,0:T(8,128)S(1)}, u32[]{:S(2)}, u32[]{:S(2)}) collective-permute-start(f32[9,16,128]{2,1,0:T(8,128)S(1)} %get-tuple-element.27), channel_id=1, source_target_pairs={{0,1},{2,3},{1,0},{3,2},{4,5},{6,7},{5,4},{7,6},{8,9},{10,11},{9,8... | collective-permute-start | bytes 221192 | tf_op jit(solution)/shard_map/ppermute | solution.py:422
  18.9 0.0 collective-permute-done.refs_4_
  18.9 0.0 collective-permute-done.1.refs_6_
  18.9 0.0 collective-permute-done.2.refs_8_
  19.0 0.0 collective-permute-done.3.refs_5_
  19.0 1.7 %collective-permute-done.4.refs_7_ = f32[9,16,128]{2,1,0:T(8,128)S(1)} collective-permute-done((f32[9,16,128]{2,1,0:T(8,128)S(1)}, f32[9,16,128]{2,1,0:T(8,128)S(1)}, u32[]{:S(2)}, u32[]{:S(2)}) %collective-permute-start.4) | collective-permute-done | bytes 73760 | tf_op jit(solution)/shard_map/ppermute | solution.py:422
  20.7 9.3 %all-to-all-start = ((f32[256,1,128]{2,1,0:T(1,128)}), f32[256,1,128]{2,1,0:T(1,128)S(1)}, u32[]{:S(2)}, u32[]{:S(2)}) async-start(f32[256,1,128]{2,1,0:T(1,128)} %bitcast.4), calls=%async_computation | async-start | bytes 262144 | tf_op jit(solution)/shard_map/all_to_all | solution.py:457
  30.0 0.4 collective-permute-start.5
  30.4 0.9 %collective-permute-done.5.refs_3_ = f32[9,16,128]{2,1,0:T(8,128)S(1)} collective-permute-done((f32[9,16,128]{2,1,0:T(8,128)S(1)}, f32[9,16,128]{2,1,0:T(8,128)S(1)}, u32[]{:S(2)}, u32[]{:S(2)}) %collective-permute-start.5) | collective-permute-done | bytes 73760 | tf_op jit(solution)/shard_map/ppermute | solution.py:422
  31.3 19.0 %near.1 = f32[64,3,128]{2,1,0:T(4,128)S(1)} custom-call(f32[3,64,128]{2,1,0:T(8,128)} %bitcast.19, f32[3,64,128]{2,1,0:T(8,128)S(1)} %get-tuple-element.29.refs_1_.masked, f32[3,64,128]{2,1,0:T(8,128)} %bitcast.14, f32[9,16,128]{2,1,0:T(8,128)S(1)} %collective-permute-done.5.refs_3_, f32[9,16,128]{2,1,0:T(8,128)S(1)} %collective-permute-done.refs_4_, ...), custom_call_target="tpu_custom_call" | custom-call | tf_op jit(solution)/shard_map/near/pallas_call | solution.py:460
  50.3 0.0 all-to-all-done
  50.3 3.9 %forces.1 = (f32[6,64,128]{2,1,0:T(8,128)S(1)}, f32[6,4,128]{2,1,0:T(4,128)S(1)}, f32[6,4,128]{2,1,0:T(4,128)S(1)}) custom-call(f32[256,128]{1,0:T(8,128)S(1)} %bitcast.12, f32[64,3,128]{2,1,0:T(4,128)S(1)} %near.1, f32[3,64,128]{2,1,0:T(8,128)S(1)} %get-tuple-element.29.refs_1_.masked, f32[3,64,128]{2,1,0:T(8,128)} %bitcast.15, f32[3,3]{1,0:T(4,128)} %stress.1, ...), custom_call_target="tpu_custom_call" | custom-call | tf_op jit(solution)/shard_map/forces/pallas_call | solution.py:473
  54.3 0.4 collective-permute-start.6
  54.7 7.9 %collective-permute-start.7 = (f32[6,4,128]{2,1,0:T(4,128)S(1)}, f32[6,4,128]{2,1,0:T(4,128)S(1)}, u32[]{:S(2)}, u32[]{:S(2)}) collective-permute-start(f32[6,4,128]{2,1,0:T(4,128)S(1)} %get-tuple-element.38), channel_id=1, source_target_pairs={{16,32},{48,64},{80,96},{112,128},{144,160},{176,192},{208,224},{3... | collective-permute-start | bytes 36872 | tf_op jit(solution)/shard_map/ppermute | solution.py:422
  62.6 4.3 %nodes.1.fields = f32[6,64,128]{2,1,0:T(8,128)S(1)} custom-call(f32[6,64,128]{2,1,0:T(8,128)S(1)} %get-tuple-element.36.values, s32[2,64,128]{2,1,0:T(8,128)} %bitcast.21, f32[3,64,128]{2,1,0:T(8,128)} %bitcast.17, f32[64,128]{1,0:T(8,128)} %bitcast.23), custom_call_target="tpu_custom_call" | custom-call | tf_op jit(solution)/shard_map/nodes/pallas_call | solution.py:482
  66.9 0.0 collective-permute-done.6.first
  67.0 0.0 collective-permute-done.7.second
  67.0 2.1 %migrate.1 = f32[6,72,128]{2,1,0:T(8,128)} custom-call(f32[6,64,128]{2,1,0:T(8,128)S(1)} %nodes.1.fields, f32[6,4,128]{2,1,0:T(4,128)S(1)} %collective-permute-done.6.first, f32[6,4,128]{2,1,0:T(4,128)S(1)} %collective-permute-done.7.second, s32[2,4,4,16]{3,2,1,0:T(4,128)} %bitcast.25), custom_call_target="tpu_custom_call" | custom-call | tf_op jit(solution)/shard_map/migrate/pallas_call | solution.py:490
Async XLA Ops:
  2.1 16.9 %collective-permute-start = (f32[9,16,128]{2,1,0:T(8,128)S(1)}, f32[9,16,128]{2,1,0:T(8,128)S(1)}, u32[]{:S(2)}, u32[]{:S(2)}) collective-permute-start(f32[9,16,128]{2,1,0:T(8,128)S(1)} %get-tuple-element.23), channel_id=1, source_target_pairs={{16,32},{48,64},{80,96},{112,128},{144,160},{176,192},{208,224},{3... | collective-permute-start | bytes 221192 | tf_op jit(solution)/shard_map/ppermute | solution.py:422
  11.1 7.8 %collective-permute-start.1 = (f32[9,16,128]{2,1,0:T(8,128)S(1)}, f32[9,16,128]{2,1,0:T(8,128)S(1)}, u32[]{:S(2)}, u32[]{:S(2)}) collective-permute-start(f32[9,16,128]{2,1,0:T(8,128)S(1)} %get-tuple-element.24), channel_id=1, source_target_pairs={{4,8},{8,4},{5,9},{9,5},{6,10},{10,6},{7,11},{11,7},{20,24},{24,20... | collective-permute-start | bytes 221192 | tf_op jit(solution)/shard_map/ppermute | solution.py:422
  11.8 7.2 %collective-permute-start.2 = (f32[9,16,128]{2,1,0:T(8,128)S(1)}, f32[9,16,128]{2,1,0:T(8,128)S(1)}, u32[]{:S(2)}, u32[]{:S(2)}) collective-permute-start(f32[9,16,128]{2,1,0:T(8,128)S(1)} %get-tuple-element.25), channel_id=1, source_target_pairs={{1,2},{2,1},{5,6},{6,5},{9,10},{10,9},{13,14},{14,13},{17,18},{18,... | collective-permute-start | bytes 221192 | tf_op jit(solution)/shard_map/ppermute | solution.py:422
  12.5 6.5 %collective-permute-start.3 = (f32[9,16,128]{2,1,0:T(8,128)S(1)}, f32[9,16,128]{2,1,0:T(8,128)S(1)}, u32[]{:S(2)}, u32[]{:S(2)}) collective-permute-start(f32[9,16,128]{2,1,0:T(8,128)S(1)} %get-tuple-element.26), channel_id=1, source_target_pairs={{0,4},{8,12},{4,0},{12,8},{1,5},{9,13},{5,1},{13,9},{2,6},{10,14},... | collective-permute-start | bytes 221192 | tf_op jit(solution)/shard_map/ppermute | solution.py:422
  15.3 5.4 %collective-permute-start.4 = (f32[9,16,128]{2,1,0:T(8,128)S(1)}, f32[9,16,128]{2,1,0:T(8,128)S(1)}, u32[]{:S(2)}, u32[]{:S(2)}) collective-permute-start(f32[9,16,128]{2,1,0:T(8,128)S(1)} %get-tuple-element.27), channel_id=1, source_target_pairs={{0,1},{2,3},{1,0},{3,2},{4,5},{6,7},{5,4},{7,6},{8,9},{10,11},{9,8... | collective-permute-start | bytes 221192 | tf_op jit(solution)/shard_map/ppermute | solution.py:422
  20.7 29.6 %all-to-all-start = ((f32[256,1,128]{2,1,0:T(1,128)}), f32[256,1,128]{2,1,0:T(1,128)S(1)}, u32[]{:S(2)}, u32[]{:S(2)}) async-start(f32[256,1,128]{2,1,0:T(1,128)} %bitcast.4), calls=%async_computation | async-start | bytes 262144 | tf_op jit(solution)/shard_map/all_to_all | solution.py:457
  30.0 1.4 %collective-permute-start.5 = (f32[9,16,128]{2,1,0:T(8,128)S(1)}, f32[9,16,128]{2,1,0:T(8,128)S(1)}, u32[]{:S(2)}, u32[]{:S(2)}) collective-permute-start(f32[9,16,128]{2,1,0:T(8,128)S(1)} %get-tuple-element.30), channel_id=1, source_target_pairs={{0,16},{32,48},{64,80},{96,112},{128,144},{160,176},{192,208},{224... | collective-permute-start | bytes 221192 | tf_op jit(solution)/shard_map/ppermute | solution.py:422
  54.3 12.7 %collective-permute-start.6 = (f32[6,4,128]{2,1,0:T(4,128)S(1)}, f32[6,4,128]{2,1,0:T(4,128)S(1)}, u32[]{:S(2)}, u32[]{:S(2)}) collective-permute-start(f32[6,4,128]{2,1,0:T(4,128)S(1)} %get-tuple-element.37), channel_id=1, source_target_pairs={{0,16},{32,48},{64,80},{96,112},{128,144},{160,176},{192,208},{224... | collective-permute-start | bytes 36872 | tf_op jit(solution)/shard_map/ppermute | solution.py:422
  54.7 12.2 %collective-permute-start.7 = (f32[6,4,128]{2,1,0:T(4,128)S(1)}, f32[6,4,128]{2,1,0:T(4,128)S(1)}, u32[]{:S(2)}, u32[]{:S(2)}) collective-permute-start(f32[6,4,128]{2,1,0:T(4,128)S(1)} %get-tuple-element.38), channel_id=1, source_target_pairs={{16,32},{48,64},{80,96},{112,128},{144,160},{176,192},{208,224},{3... | collective-permute-start | bytes 36872 | tf_op jit(solution)/shard_map/ppermute | solution.py:422

commit v7 on v6

--- a/solution.py
+++ b/solution.py
@@ -331,7 +331,7 @@
             preferred_element_type=F32,
         )
 
-    total = lax.fori_loop(0, CELLS // STEP_CELLS, scatter, jnp.zeros((48, LANES), F32))
+    total = lax.fori_loop(0, CELLS // STEP_CELLS, scatter, jnp.zeros((48, LANES), F32), unroll=2)
     even = index_x % 2 == 0
     for a in range(3):
         force = total[8 * a : 8 * a + 8] + total[24 + 8 * a : 32 + 8 * a]
@@ -371,7 +371,7 @@
         )
         return carry
 
-    lax.fori_loop(0, CELLS // STEP_CELLS, scatter, 0, unroll=1)
+    lax.fori_loop(0, CELLS // STEP_CELLS, scatter, 0, unroll=2)
     for a in range(3):
         force = sums[pl.ds(32 * a, 32), :] + sums[pl.ds(96 + 32 * a, 32), :]
         fields[3 + a, pl.ds(0, 32, stride=2), :] = force[:, :LANES]

time: 69.4 us -> 68.8 us (level)
  no operation moved by 1% of the time
where the time goes in v7:
time: 68.8 us; the launch traced here: 68.4 us
  starting transfers between devices  34.9 us (51%)
  Pallas kernels  30.8 us (45%)
  waiting for transfers between devices  2.65 us (4%)
    ppermute x8, starting transfers between devices, exchanged(): return lax.ppermute(array, axis, pairs + [(b, a) for a, b in pairs])  25.6 us
    pallas_call x1, Pallas kernels, shards(): pl.pallas_call(near_kernel, in_specs=[vmem] * 9, out_shape=shape(CELLS, 3...  19 us
    all_to_all x1, starting transfers between devices, shards(): lax.all_to_all(moments.reshape(256, 1, LANES), AXES, 0, 0, tiled=True)  9.28 us
    pallas_call x1, Pallas kernels, shards(): pl.pallas_call(node_kernel, in_specs=[vmem] * 4, out_shape=shape(6, 64, L...  3.97 us
    pallas_call x1, Pallas kernels, shards(): pl.pallas_call(force_kernel, in_specs=[vmem] * 4 + [smem] + [vmem] * 3, o...  3.66 us
    ppermute x8, waiting for transfers between devices, exchanged(): return lax.ppermute(array, axis, pairs + [(b, a) for a, b in pairs])  2.65 us
    pallas_call x1, Pallas kernels, shards(): pl.pallas_call(prepare_kernel, in_specs=[vmem, vmem, vmem, smem], out_sha...  2.09 us
    pallas_call x1, Pallas kernels, shards(): pl.pallas_call(migrate_kernel, in_specs=[vmem] * 3 + [smem], out_shape=ja...  2.06 us
  transfers between devices with their start and end apart: 9, of which 2 were waited for; matrix products, arithmetic and copies ran while one was open for 0% of the time, Pallas kernels for 34%

profile of v7, /device:TPU:25, one launch (start us, length us, event | category | flops | bytes accessed | tf_op | source)
XLA Modules:
  0.0 68.4 jit_solution(17663560868883484756)
XLA Ops:
  0.0 2.1 %prepare.1 = (f32[3,64,128]{2,1,0:T(8,128)S(1)}, f32[256,128]{1,0:T(8,128)}, f32[9,16,128]{2,1,0:T(8,128)S(1)}, f32[9,16,128]{2,1,0:T(8,128)S(1)}, f32[9,16,128]...) custom-call(f32[3,64,128]{2,1,0:T(8,128)} %bitcast.18, ...), custom_call_target="tpu_custom_call" | custom-call | tf_op jit(solution)/shard_map/prepare/pallas_call | solution.py:444
  2.1 9.0 %collective-permute-start = (f32[9,16,128]{2,1,0:T(8,128)S(1)}, f32[9,16,128]{2,1,0:T(8,128)S(1)}, u32[]{:S(2)}, u32[]{:S(2)}) collective-permute-start(f32[9,16,128]{2,1,0:T(8,128)S(1)} %get-tuple-element.23), channel_id=1, source_target_pairs={{16,32},{48,64},{80,96},{112,128},{144,160},{176,192},{208,224},{3... | collective-permute-start | bytes 221192 | tf_op jit(solution)/shard_map/ppermute | solution.py:422
  11.1 0.7 collective-permute-start.1
  11.8 0.7 collective-permute-start.2
  12.5 2.8 %collective-permute-start.3 = (f32[9,16,128]{2,1,0:T(8,128)S(1)}, f32[9,16,128]{2,1,0:T(8,128)S(1)}, u32[]{:S(2)}, u32[]{:S(2)}) collective-permute-start(f32[9,16,128]{2,1,0:T(8,128)S(1)} %get-tuple-element.26), channel_id=1, source_target_pairs={{0,4},{8,12},{4,0},{12,8},{1,5},{9,13},{5,1},{13,9},{2,6},{10,14},... | collective-permute-start | bytes 221192 | tf_op jit(solution)/shard_map/ppermute | solution.py:422
  15.3 3.7 %collective-permute-start.4 = (f32[9,16,128]{2,1,0:T(8,128)S(1)}, f32[9,16,128]{2,1,0:T(8,128)S(1)}, u32[]{:S(2)}, u32[]{:S(2)}) collective-permute-start(f32[9,16,128]{2,1,0:T(8,128)S(1)} %get-tuple-element.27), channel_id=1, source_target_pairs={{0,1},{2,3},{1,0},{3,2},{4,5},{6,7},{5,4},{7,6},{8,9},{10,11},{9,8... | collective-permute-start | bytes 221192 | tf_op jit(solution)/shard_map/ppermute | solution.py:422
  18.9 0.0 collective-permute-done.refs_4_
  18.9 0.0 collective-permute-done.1.refs_6_
  18.9 0.0 collective-permute-done.2.refs_8_
  19.0 0.0 collective-permute-done.3.refs_5_
  19.0 1.7 %collective-permute-done.4.refs_7_ = f32[9,16,128]{2,1,0:T(8,128)S(1)} collective-permute-done((f32[9,16,128]{2,1,0:T(8,128)S(1)}, f32[9,16,128]{2,1,0:T(8,128)S(1)}, u32[]{:S(2)}, u32[]{:S(2)}) %collective-permute-start.4) | collective-permute-done | bytes 73760 | tf_op jit(solution)/shard_map/ppermute | solution.py:422
  20.7 9.3 %all-to-all-start = ((f32[256,1,128]{2,1,0:T(1,128)}), f32[256,1,128]{2,1,0:T(1,128)S(1)}, u32[]{:S(2)}, u32[]{:S(2)}) async-start(f32[256,1,128]{2,1,0:T(1,128)} %bitcast.4), calls=%async_computation | async-start | bytes 262144 | tf_op jit(solution)/shard_map/all_to_all | solution.py:457
  30.0 0.4 collective-permute-start.5
  30.4 0.9 %collective-permute-done.5.refs_3_ = f32[9,16,128]{2,1,0:T(8,128)S(1)} collective-permute-done((f32[9,16,128]{2,1,0:T(8,128)S(1)}, f32[9,16,128]{2,1,0:T(8,128)S(1)}, u32[]{:S(2)}, u32[]{:S(2)}) %collective-permute-start.5) | collective-permute-done | bytes 73760 | tf_op jit(solution)/shard_map/ppermute | solution.py:422
  31.3 19.0 %near.1 = f32[64,3,128]{2,1,0:T(4,128)S(1)} custom-call(f32[3,64,128]{2,1,0:T(8,128)} %bitcast.19, f32[3,64,128]{2,1,0:T(8,128)S(1)} %get-tuple-element.29.refs_1_.masked, f32[3,64,128]{2,1,0:T(8,128)} %bitcast.14, f32[9,16,128]{2,1,0:T(8,128)S(1)} %collective-permute-done.5.refs_3_, f32[9,16,128]{2,1,0:T(8,128)S(1)} %collective-permute-done.refs_4_, ...), custom_call_target="tpu_custom_call" | custom-call | tf_op jit(solution)/shard_map/near/pallas_call | solution.py:460
  50.3 0.0 all-to-all-done
  50.3 3.7 %forces.1 = (f32[6,64,128]{2,1,0:T(8,128)S(1)}, f32[6,4,128]{2,1,0:T(4,128)S(1)}, f32[6,4,128]{2,1,0:T(4,128)S(1)}) custom-call(f32[256,128]{1,0:T(8,128)S(1)} %bitcast.12, f32[64,3,128]{2,1,0:T(4,128)S(1)} %near.1, f32[3,64,128]{2,1,0:T(8,128)S(1)} %get-tuple-element.29.refs_1_.masked, f32[3,64,128]{2,1,0:T(8,128)} %bitcast.15, f32[3,3]{1,0:T(4,128)} %stress.1, ...), custom_call_target="tpu_custom_call" | custom-call | tf_op jit(solution)/shard_map/forces/pallas_call | solution.py:473
  54.0 0.4 collective-permute-start.6
  54.5 7.9 %collective-permute-start.7 = (f32[6,4,128]{2,1,0:T(4,128)S(1)}, f32[6,4,128]{2,1,0:T(4,128)S(1)}, u32[]{:S(2)}, u32[]{:S(2)}) collective-permute-start(f32[6,4,128]{2,1,0:T(4,128)S(1)} %get-tuple-element.38), channel_id=1, source_target_pairs={{16,32},{48,64},{80,96},{112,128},{144,160},{176,192},{208,224},{3... | collective-permute-start | bytes 36872 | tf_op jit(solution)/shard_map/ppermute | solution.py:422
  62.4 4.0 %nodes.1.fields = f32[6,64,128]{2,1,0:T(8,128)S(1)} custom-call(f32[6,64,128]{2,1,0:T(8,128)S(1)} %get-tuple-element.36.values, s32[2,64,128]{2,1,0:T(8,128)} %bitcast.21, f32[3,64,128]{2,1,0:T(8,128)} %bitcast.17, f32[64,128]{1,0:T(8,128)} %bitcast.23), custom_call_target="tpu_custom_call" | custom-call | tf_op jit(solution)/shard_map/nodes/pallas_call | solution.py:482
  66.3 0.0 collective-permute-done.6.first
  66.4 0.0 collective-permute-done.7.second
  66.4 2.1 %migrate.1 = f32[6,72,128]{2,1,0:T(8,128)} custom-call(f32[6,64,128]{2,1,0:T(8,128)S(1)} %nodes.1.fields, f32[6,4,128]{2,1,0:T(4,128)S(1)} %collective-permute-done.6.first, f32[6,4,128]{2,1,0:T(4,128)S(1)} %collective-permute-done.7.second, s32[2,4,4,16]{3,2,1,0:T(4,128)} %bitcast.25), custom_call_target="tpu_custom_call" | custom-call | tf_op jit(solution)/shard_map/migrate/pallas_call | solution.py:490
Async XLA Ops:
  2.1 16.9 %collective-permute-start = (f32[9,16,128]{2,1,0:T(8,128)S(1)}, f32[9,16,128]{2,1,0:T(8,128)S(1)}, u32[]{:S(2)}, u32[]{:S(2)}) collective-permute-start(f32[9,16,128]{2,1,0:T(8,128)S(1)} %get-tuple-element.23), channel_id=1, source_target_pairs={{16,32},{48,64},{80,96},{112,128},{144,160},{176,192},{208,224},{3... | collective-permute-start | bytes 221192 | tf_op jit(solution)/shard_map/ppermute | solution.py:422
  11.1 7.8 %collective-permute-start.1 = (f32[9,16,128]{2,1,0:T(8,128)S(1)}, f32[9,16,128]{2,1,0:T(8,128)S(1)}, u32[]{:S(2)}, u32[]{:S(2)}) collective-permute-start(f32[9,16,128]{2,1,0:T(8,128)S(1)} %get-tuple-element.24), channel_id=1, source_target_pairs={{4,8},{8,4},{5,9},{9,5},{6,10},{10,6},{7,11},{11,7},{20,24},{24,20... | collective-permute-start | bytes 221192 | tf_op jit(solution)/shard_map/ppermute | solution.py:422
  11.8 7.2 %collective-permute-start.2 = (f32[9,16,128]{2,1,0:T(8,128)S(1)}, f32[9,16,128]{2,1,0:T(8,128)S(1)}, u32[]{:S(2)}, u32[]{:S(2)}) collective-permute-start(f32[9,16,128]{2,1,0:T(8,128)S(1)} %get-tuple-element.25), channel_id=1, source_target_pairs={{1,2},{2,1},{5,6},{6,5},{9,10},{10,9},{13,14},{14,13},{17,18},{18,... | collective-permute-start | bytes 221192 | tf_op jit(solution)/shard_map/ppermute | solution.py:422
  12.5 6.5 %collective-permute-start.3 = (f32[9,16,128]{2,1,0:T(8,128)S(1)}, f32[9,16,128]{2,1,0:T(8,128)S(1)}, u32[]{:S(2)}, u32[]{:S(2)}) collective-permute-start(f32[9,16,128]{2,1,0:T(8,128)S(1)} %get-tuple-element.26), channel_id=1, source_target_pairs={{0,4},{8,12},{4,0},{12,8},{1,5},{9,13},{5,1},{13,9},{2,6},{10,14},... | collective-permute-start | bytes 221192 | tf_op jit(solution)/shard_map/ppermute | solution.py:422
  15.3 5.4 %collective-permute-start.4 = (f32[9,16,128]{2,1,0:T(8,128)S(1)}, f32[9,16,128]{2,1,0:T(8,128)S(1)}, u32[]{:S(2)}, u32[]{:S(2)}) collective-permute-start(f32[9,16,128]{2,1,0:T(8,128)S(1)} %get-tuple-element.27), channel_id=1, source_target_pairs={{0,1},{2,3},{1,0},{3,2},{4,5},{6,7},{5,4},{7,6},{8,9},{10,11},{9,8... | collective-permute-start | bytes 221192 | tf_op jit(solution)/shard_map/ppermute | solution.py:422
  20.7 29.6 %all-to-all-start = ((f32[256,1,128]{2,1,0:T(1,128)}), f32[256,1,128]{2,1,0:T(1,128)S(1)}, u32[]{:S(2)}, u32[]{:S(2)}) async-start(f32[256,1,128]{2,1,0:T(1,128)} %bitcast.4), calls=%async_computation | async-start | bytes 262144 | tf_op jit(solution)/shard_map/all_to_all | solution.py:457
  30.0 1.4 %collective-permute-start.5 = (f32[9,16,128]{2,1,0:T(8,128)S(1)}, f32[9,16,128]{2,1,0:T(8,128)S(1)}, u32[]{:S(2)}, u32[]{:S(2)}) collective-permute-start(f32[9,16,128]{2,1,0:T(8,128)S(1)} %get-tuple-element.30), channel_id=1, source_target_pairs={{0,16},{32,48},{64,80},{96,112},{128,144},{160,176},{192,208},{224... | collective-permute-start | bytes 221192 | tf_op jit(solution)/shard_map/ppermute | solution.py:422
  54.0 12.3 %collective-permute-start.6 = (f32[6,4,128]{2,1,0:T(4,128)S(1)}, f32[6,4,128]{2,1,0:T(4,128)S(1)}, u32[]{:S(2)}, u32[]{:S(2)}) collective-permute-start(f32[6,4,128]{2,1,0:T(4,128)S(1)} %get-tuple-element.37), channel_id=1, source_target_pairs={{0,16},{32,48},{64,80},{96,112},{128,144},{160,176},{192,208},{224... | collective-permute-start | bytes 36872 | tf_op jit(solution)/shard_map/ppermute | solution.py:422
  54.5 11.9 %collective-permute-start.7 = (f32[6,4,128]{2,1,0:T(4,128)S(1)}, f32[6,4,128]{2,1,0:T(4,128)S(1)}, u32[]{:S(2)}, u32[]{:S(2)}) collective-permute-start(f32[6,4,128]{2,1,0:T(4,128)S(1)} %get-tuple-element.38), channel_id=1, source_target_pairs={{16,32},{48,64},{80,96},{112,128},{144,160},{176,192},{208,224},{3... | collective-permute-start | bytes 36872 | tf_op jit(solution)/shard_map/ppermute | solution.py:422
